TPU v7x, 256 devices: a whole 4x4x8 slice. The times are simulated.
256 devices in a mesh: row: 8 (over z_hi, core), col: 32 (over x, z_lo, y).
Axes of the slice: x: 4, y: 4, z: 8 (z_hi: 4, z_lo: 2; z = z_hi * 2 + z_lo), core: 2. Of those that a mesh axis runs over, the one named last changes fastest.
Arguments:
- features: bfloat16 [131072, 128], P(('row', 'col')), may hold values from -6 to 6
- weight: bfloat16 [128, 128], replicated, may hold values from -0.5 to 0.5
- bias: float32 [128], replicated, may hold values from -3 to 3
- cotangent: bfloat16 [131072, 128], P(('row', 'col')), may hold values from -6 to 6
- block_count: int32 [8, 32], P('row', 'col'), may hold values from 64 to 512
- block_rows: int32 [8, 32, 512], P('row', 'col'), may hold values from 0 to 127
- block_cols: int32 [8, 32, 512], P('row', 'col'), may hold values from 0 to 31
- edge_offsets: int32 [8, 32, 512, 128], P('row', 'col'), may hold values from 0 to 16383, as said below
- edge_weight: bfloat16 [8, 32, 512, 128], P('row', 'col'), may hold values from 0.0099487305 to 0.099609375
Outputs:
- output: bfloat16 [131072, 128], P(('row', 'col'))
- grad_features: bfloat16 [131072, 128], P(('row', 'col'))
- grad_weight: float32 [128, 128], replicated
- grad_bias: float32 [128], replicated
Inputs may be any that keep to these rules, and one draw needn't show every extreme that they name: `edge_offsets`: the offsets within one slot are distinct.
All inputs are finite; a program needn't handle non-finite values.
Results may differ from a plain program's by a relative error of at most 0.013.
The roundings to bfloat16 on the way count: a program that leaves them out, or rounds other values in their place, can miss the bound.
Values may be sent and summed in bfloat16 or wider, within the bound.
A program may use at most 128 MiB of HBM per device.

v0:
```python
import jax
import jax.numpy as jnp
from jax import lax
from jax.sharding import PartitionSpec as P


def shards(
    features,
    weight,
    bias,
    cotangent,
    block_count,
    block_rows,
    block_cols,
    edge_offsets,
    edge_weight,
):
    node_dev, width = features.shape
    n_row = lax.axis_size("row")
    n_col = lax.axis_size("col")
    slots = block_rows.shape[2]
    batch = min(64, slots)
    count = block_count[0, 0]
    turns = (count + batch - 1) // batch
    brow = block_rows[0, 0]
    bcol = block_cols[0, 0]
    offsets = edge_offsets[0, 0]
    weights = edge_weight[0, 0]
    lanes = jnp.arange(batch, dtype=jnp.int32)
    within = jnp.arange(128, dtype=jnp.int32)
    row_blocks = node_dev * n_col // 128
    col_blocks = node_dev * n_row // 128
    row_ids = jnp.arange(row_blocks, dtype=jnp.int32)
    col_ids = jnp.arange(col_blocks, dtype=jnp.int32)
    projected = jnp.dot(features, weight, preferred_element_type=jnp.float32).astype(jnp.bfloat16)
    panel = lax.all_gather(projected, "row", axis=0, tiled=True).reshape(-1, 128, width)

    def forward_step(i, carry):
        stored, totals = carry
        start = i * batch
        offs = lax.dynamic_slice_in_dim(offsets, start, batch, 0)
        vals = lax.dynamic_slice_in_dim(weights, start, batch, 0).astype(jnp.float32)
        vals = jnp.where((start + lanes < count)[:, None], vals, 0.0)
        left = jnp.where((offs // 128)[:, :, None] == within, vals[:, :, None], 0.0).astype(
            jnp.bfloat16
        )
        right = ((offs % 128)[:, :, None] == within).astype(jnp.bfloat16)
        dense = jnp.einsum("bei,bej->bij", left, right, preferred_element_type=jnp.float32).astype(
            jnp.bfloat16
        )
        stored = lax.dynamic_update_slice_in_dim(stored, dense, start, 0)
        rows_here = lax.dynamic_slice_in_dim(brow, start, batch, 0)
        cols_here = lax.dynamic_slice_in_dim(bcol, start, batch, 0)
        product = jnp.einsum(
            "bij,bjf->bif", dense, panel[cols_here], preferred_element_type=jnp.float32
        )
        select = (rows_here[:, None] == row_ids).astype(jnp.float32)
        added = jnp.einsum(
            "br,bif->rif",
            select,
            product,
            precision=lax.Precision.HIGHEST,
            preferred_element_type=jnp.float32,
        )
        return (stored, totals + added)

    stored0 = jnp.zeros((slots, 128, 128), jnp.bfloat16)
    totals0 = jnp.zeros((row_blocks, 128, width), jnp.float32)
    stored, totals = lax.fori_loop(0, turns, forward_step, (stored0, totals0))
    totals = totals.reshape(-1, width)
    own = lax.psum_scatter(totals, "col", scatter_dimension=0, tiled=True)
    pre = own + bias
    output = jnp.maximum(pre, 0.0).astype(jnp.bfloat16)
    grad_own = jnp.where(pre > 0, cotangent.astype(jnp.float32), 0.0).astype(jnp.bfloat16)
    grad_panel = lax.all_gather(grad_own, "col", axis=0, tiled=True)
    grad_blocks = grad_panel.reshape(-1, 128, width)

    def backward_step(i, acc):
        start = i * batch
        dense = lax.dynamic_slice_in_dim(stored, start, batch, 0)
        rows_here = lax.dynamic_slice_in_dim(brow, start, batch, 0)
        cols_here = lax.dynamic_slice_in_dim(bcol, start, batch, 0)
        product = jnp.einsum(
            "bij,bif->bjf", dense, grad_blocks[rows_here], preferred_element_type=jnp.float32
        )
        select = (cols_here[:, None] == col_ids).astype(jnp.float32)
        added = jnp.einsum(
            "bc,bjf->cjf",
            select,
            product,
            precision=lax.Precision.HIGHEST,
            preferred_element_type=jnp.float32,
        )
        return acc + added

    acc0 = jnp.zeros((col_blocks, 128, width), jnp.float32)
    acc = lax.fori_loop(0, turns, backward_step, acc0)
    grad_proj = lax.psum_scatter(
        acc.reshape(-1, width), "row", scatter_dimension=0, tiled=True
    ).astype(jnp.bfloat16)
    grad_features = lax.dot_general(
        grad_proj, weight, (((1,), (1,)), ((), ())), preferred_element_type=jnp.float32
    ).astype(jnp.bfloat16)
    local_weight = lax.dot_general(
        features, grad_proj, (((0,), (0,)), ((), ())), preferred_element_type=jnp.float32
    )
    local_bias = jnp.sum(grad_own.astype(jnp.float32), axis=0)
    total_weight, total_bias = lax.psum((local_weight, local_bias), ("row", "col"))
    scale = (node_dev * n_row * n_col) ** (-0.5)
    return (output, grad_features, total_weight * scale, total_bias * scale)


def solution(mesh):
    return jax.shard_map(
        shards,
        mesh=mesh,
        in_specs=(
            P(("row", "col"), None),
            P(),
            P(),
            P(("row", "col"), None),
            P("row", "col"),
            P("row", "col", None),
            P("row", "col", None),
            P("row", "col", None, None),
            P("row", "col", None, None),
        ),
        out_specs=(P(("row", "col"), None), P(("row", "col"), None), P(), P()),
        check_vma=False,
    )
```

profile of v0, /device:TPU:1, one launch (start us, length us, event | category | flops | bytes accessed | tf_op | source)
XLA Modules:
  0.0 1007.0 jit_solution(10887614581579675863)
XLA Ops:
  7.2 0.8 copy-done
  8.1 1.6 convolution_convert_fusion.1
  10.4 34.3 %all-gather.3.cloned.1.call-done = bf16[4096,128]{1,0:T(8,128)(2,1)} async-done(((bf16[512,128]{1,0:T(8,128)(2,1)}), bf16[4096,128]{1,0:T(8,128)(2,1)}) %all-gather.3.cloned.1.call-update) | async-done | bytes 1048592 | tf_op jit(solution)/shard_map/all_gather | solution.py:36
  44.7 6.3 broadcast_in_dim.84
  51.0 4.3 broadcast_in_dim.85
  55.3 21.7 %while.29 = (s32[]{:T(128)}, bf16[512,128,128]{2,1,0:T(8,128)(2,1)}, f32[128,128,128]{2,0,1:T(8,128)}, s32[]{:T(128)}, s32[512,128]{1,0:T(8,128)}, /*index=5*/s3...) while((s32[]{:T(128)}, ...), condition=%wide.region_1.2_spmd.clone.clone, body=%wide.region_0.1_spmd.clone.clone.sunk | while | flops 2154005760 | bytes 38017104 | solution.py:69
  58.3 3.6 constant_dynamic-update-slice_fusion.2
  62.0 0.9 gather_fusion.1
  62.9 2.3 fusion.69
  65.3 11.7 %fusion.70 = f32[128,128,128]{2,0,1:T(8,128)} fusion(f32[128,128,128]{2,0,1:T(8,128)} %get-tuple-element.493, f32[64,128,128]{2,1,0:T(8,128)S(1)} %fusion.69, s32[64]{0:T(128)S(1)} %dynamic_slice.84), kind=kOutput, calls=%fused_computation.22.clone.1 | convolution fusion | flops 1612718080 | bytes 20971776 | tf_op jit(solution)/shard_map/while/body/br,bif->rif/dot_general | solution.py:58
  77.0 11.5 %copy.17 = f32[128,128,128]{2,1,0:T(8,128)} copy(f32[128,128,128]{2,0,1:T(8,128)} %get-tuple-element.240) | data formatting | bytes 16777216 | tf_op jit(solution)/shard_map/while | solution.py:69
  88.5 309.5 %reduce-scatter.3.cloned.1.call-done = f32[512,128]{1,0:T(8,128)} async-done(((f32[16384,128]{1,0:T(8,128)}), f32[512,128]{1,0:T(8,128)}) %reduce-scatter.3.cloned.1.call-update) | async-done | bytes 262160 | tf_op jit(solution)/shard_map/reduce_scatter | solution.py:71
  398.0 1.7 convert_reduce_fusion
  399.8 158.8 %all-gather.5.cloned.1.call-done = bf16[16384,128]{1,0:T(8,128)(2,1)} async-done(((bf16[512,128]{1,0:T(8,128)(2,1)}), bf16[16384,128]{1,0:T(8,128)(2,1)}) %all-gather.5.cloned.1.call-update) | async-done | bytes 4194320 | tf_op jit(solution)/shard_map/all_gather | solution.py:75
  558.6 1.6 broadcast_in_dim.86
  560.2 12.7 %while.28 = (s32[]{:T(128)}, f32[32,128,128]{2,0,1:T(8,128)}, s32[]{:T(128)}, s32[512]{0:T(512)S(1)}, bf16[512,128,128]{2,1,0:T(8,128)(2,1)}, /*index=5*/s32[512...) while((s32[]{:T(128)}, f32[32,128,128]{2,0,1:T(8,128)}, ...), condition=%wide.region_4.5_spmd.clone, body=%wide.region_3.4_spmd.clone.sunk | while | flops 671616192 | bytes 20977576 | solution.py:97
  560.3 3.1 gather_fusion
  563.4 2.5 fusion.62
  566.0 7.0 fusion.63
  572.9 4.1 copy.18
  577.2 184.7 %psum.15 = f32[128]{0:T(128)S(1)} all-reduce(f32[128]{0:T(128)S(1)} %get-tuple-element.358), channel_id=1, replica_groups=mesh['row'=8,'col'=32] {'row','col'}, use_global_device_ids=true, to_apply=%region_8.9 | all-reduce | flops 128 | bytes 1024 | tf_op jit(solution)/shard_map/psum | solution.py:108
  762.4 1.8 convolution_bitcast_fusion
  764.2 1.8 convolution_convert_fusion
  766.0 232.8 %all-reduce.2.cloned.1.call-done = f32[128,128]{0,1:T(8,128)} async-done(((f32[128,128]{0,1:T(8,128)}), f32[128,128]{0,1:T(8,128)}) %all-reduce.2.cloned.1.call-update) | async-done | bytes 65552 | tf_op jit(solution)/shard_map/psum | solution.py:108
  (37 shorter events, 5.8 us)
Async XLA Ops:
  7.2 0.9 copy-start
  7.2 37.5 %all-gather.3.cloned.1.call-start = ((), (), s32[]{:S(2)}) async-start(), calls=%async_computation.2 | async-start | bytes 1179648 | tf_op jit(solution)/shard_map/all_gather | solution.py:36
  9.7 388.3 %reduce-scatter.3.cloned.1.call-start = ((), (), s32[]{:S(2)}) async-start(), calls=%async_computation.3 | async-start | bytes 8650752 | tf_op jit(solution)/shard_map/reduce_scatter | solution.py:71
  51.0 4.3 copy-start.1
  51.0 4.3 copy-start.5
  51.0 4.3 copy-start.6
  88.4 309.5 %copy-start.2 = (bf16[512,128]{1,0:T(8,128)(2,1)S(1)}, bf16[512,128]{1,0:T(8,128)(2,1)}, u32[]{:S(2)}) copy-start(bf16[512,128]{1,0:T(8,128)(2,1)} %param.16) | copy-start | bytes 393220
  88.4 309.5 %copy-start.4 = (f32[128]{0:T(128)S(1)}, f32[128]{0:T(128)}, u32[]{:S(2)}) copy-start(f32[128]{0:T(128)} %param.15) | copy-start | bytes 1540
  88.5 470.1 %all-gather.5.cloned.1.call-start = ((), (), s32[]{:S(2)}) async-start(), calls=%async_computation.4 | async-start | bytes 4325376 | tf_op jit(solution)/shard_map/all_gather | solution.py:75
  399.7 362.7 %reduce-scatter.5.cloned.1.call-start = ((), (), s32[]{:S(2)}) async-start(), calls=%async_computation.5 | async-start | bytes 2359296 | tf_op jit(solution)/shard_map/reduce_scatter | solution.py:98
  572.9 191.3 %copy-start.3 = (bf16[128,128]{1,0:T(8,128)(2,1)S(1)}, bf16[128,128]{1,0:T(8,128)(2,1)}, u32[]{:S(2)}) copy-start(bf16[128,128]{1,0:T(8,128)(2,1)} %param.14) | copy-start | bytes 98308
  577.1 421.8 %all-reduce.2.cloned.1.call-start = ((), (), s32[]{:S(2)}) async-start(), calls=%async_computation.6 | async-start | bytes 131072 | tf_op jit(solution)/shard_map/psum | solution.py:108
Sparse Core Ops, SparseCore 0:
  10.4 34.2 all-gather.2
  88.6 309.3 reduce-scatter.2
  400.4 158.2 all-gather.4
  577.2 148.6 reduce-scatter.4
  764.4 234.4 all-reduce.1
where the time goes:
time: 1010 us
  waiting for transfers between devices  736 us (73%)
  blocking collectives  185 us (18%)
  local copies, waits for them, and re-layouts  33.6 us (3%)
  matrix products  32.1 us (3%)
  between operations  14.5 us (1%)
    reduce_scatter x1, waiting for transfers between devices, shards(): own = lax.psum_scatter(totals, 'col', scatter_dimension=0, tiled=True)  309 us
    psum x1, waiting for transfers between devices, shards(): lax.psum((local_weight, local_bias), ('row', 'col'))  233 us
    psum x1, blocking collectives, shards(): lax.psum((local_weight, local_bias), ('row', 'col'))  185 us
    all_gather x1, waiting for transfers between devices, shards(): grad_panel = lax.all_gather(grad_own, 'col', axis=0, tiled=True)  159 us
    all_gather x1, waiting for transfers between devices, shards(): lax.all_gather(projected, 'row', axis=0, tiled=True).reshape(-1, 128, width)  34.3 us
  transfers between devices with their start and end apart: 5, of which 4 were waited for; matrix products, arithmetic and copies ran while one was open for 0% of the time, Pallas kernels for 0%

commit v1 on v0

v1 whole, which is shorter than its diff:
```python
import functools

import jax
import jax.numpy as jnp
from jax import lax
from jax.experimental import pallas as pl
from jax.experimental.pallas import tpu as pltpu
from jax.sharding import PartitionSpec as P

MESH = pl.DeviceIdType.MESH
F32 = jnp.float32
BF16 = jnp.bfloat16
BATCH = 16
PIECE = 24


def place():
    r = lax.axis_index("row")
    c = lax.axis_index("col")
    return lax.div(c, 8), lax.rem(lax.div(c, 4), 2), lax.rem(c, 4), lax.div(r, 2), lax.rem(r, 2)


def shifted(here, dx=0, dz=0, dy=0, dh=0, dk=0):
    x, z, y, h, k = here
    x, z, y = lax.rem(x + dx, 4), lax.rem(z + dz, 2), lax.rem(y + dy, 4)
    h, k = lax.rem(h + dh, 4), lax.rem(k + dk, 2)
    return (h * 2 + k, x * 8 + z * 4 + y)


def densify_kernel(count_ref, off_ref, w_ref, d_ref):
    start = pl.program_id(0) * BATCH
    off = off_ref[...]
    hi = lax.shift_right_logical(off, 7).astype(F32)
    lo = lax.bitwise_and(off, 127).astype(F32)
    slot = start + lax.broadcasted_iota(jnp.int32, off.shape, 0)
    w = jnp.where(slot < count_ref[0], w_ref[...].astype(F32), 0.0)
    ids = (
        lax.broadcasted_iota(jnp.int32, (8, 16, 128), 0) * 16
        + lax.broadcasted_iota(jnp.int32, (8, 16, 128), 1)
    ).astype(F32).astype(BF16)
    one = jnp.ones((8, 16, 128), BF16)
    zero = jnp.zeros((8, 16, 128), BF16)

    def row(a, s):
        return jnp.broadcast_to(a[s : s + 1], (16, 128)).astype(BF16)[None]

    for s in range(BATCH):
        left = jnp.where(ids == row(hi, s), jnp.broadcast_to(row(w, s), (8, 16, 128)), zero)
        right = jnp.where(ids == row(lo, s), one, zero)
        d_ref[s] = lax.dot_general(
            right.reshape(128, 128),
            left.reshape(128, 128),
            (((1,), (1,)), ((), ())),
            preferred_element_type=F32,
        ).astype(BF16)


def densify(count, offsets, weights):
    slots = offsets.shape[0]
    return pl.pallas_call(
        densify_kernel,
        grid_spec=pltpu.PrefetchScalarGridSpec(
            num_scalar_prefetch=1,
            grid=(slots // BATCH,),
            in_specs=[
                pl.BlockSpec((BATCH, 128), lambda i, n: (i, 0)),
                pl.BlockSpec((BATCH, 128), lambda i, n: (i, 0)),
            ],
            out_specs=pl.BlockSpec((BATCH, 128, 128), lambda i, n: (i, 0, 0)),
        ),
        out_shape=jax.ShapeDtypeStruct((slots, 128, 128), BF16),
        compiler_params=pltpu.CompilerParams(vmem_limit_bytes=16 << 20),
        cost_estimate=pl.CostEstimate(
            flops=slots * 128**3 * 2 * 8, bytes_accessed=slots * 128 * 262, transcendentals=0
        ),
        name="densify",
    )(count, offsets, weights)


def forward_kernel(count_ref, row_ref, col_ref, d_ref, x_ref, t_ref):
    step = pl.program_id(0)

    @pl.when(step == 0)
    def _():
        t_ref[...] = jnp.zeros_like(t_ref)

    @pl.when(step * BATCH < count_ref[0])
    def _():
        for s in range(BATCH):
            r = row_ref[step * BATCH + s]
            c = col_ref[step * BATCH + s]
            t_ref[r] += jnp.dot(x_ref[c], d_ref[s], preferred_element_type=F32)


def backward_kernel(count_ref, row_ref, col_ref, d_ref, y_ref, t_ref):
    step = pl.program_id(0)

    @pl.when(step == 0)
    def _():
        t_ref[...] = jnp.zeros_like(t_ref)

    @pl.when(step * BATCH < count_ref[0])
    def _():
        for s in range(BATCH):
            r = row_ref[step * BATCH + s]
            c = col_ref[step * BATCH + s]
            t_ref[c] += jnp.dot(d_ref[s], y_ref[r], preferred_element_type=F32)


def block_sums(kernel, name, count, brow, bcol, dense, panel, blocks):
    slots = dense.shape[0]
    return pl.pallas_call(
        kernel,
        grid_spec=pltpu.PrefetchScalarGridSpec(
            num_scalar_prefetch=3,
            grid=(slots // BATCH,),
            in_specs=[
                pl.BlockSpec((BATCH, 128, 128), lambda i, *_: (i, 0, 0)),
                pl.BlockSpec(memory_space=pltpu.VMEM),
            ],
            out_specs=pl.BlockSpec(memory_space=pltpu.VMEM),
        ),
        out_shape=jax.ShapeDtypeStruct((blocks, 128, 128), F32),
        compiler_params=pltpu.CompilerParams(vmem_limit_bytes=24 << 20),
        cost_estimate=pl.CostEstimate(
            flops=slots * 128**3 * 2, bytes_accessed=slots * 128 * 256, transcendentals=0
        ),
        name=name,
    )(count, brow, bcol, dense, panel)


class Copies:
    def __init__(self, send, recv):
        self.send, self.recv, self.used = send, recv, 0

    def start(self, src, dst, device):
        copy = pltpu.make_async_remote_copy(
            src_ref=src,
            dst_ref=dst,
            send_sem=self.send.at[self.used],
            recv_sem=self.recv.at[self.used],
            device_id=device,
            device_id_type=MESH,
        )
        self.used += 1
        copy.start()
        return copy


def ring_sum(copies, pick, me, plus, minus, near, far, total):
    p1, p2, p3 = lax.rem(me + 1, 4), lax.rem(me + 2, 4), lax.rem(me + 3, 4)
    first = [
        copies.start(pick(p2, 0), near.at[0], plus),
        copies.start(pick(p2, 1), near.at[1], minus),
        copies.start(pick(p1, 1), far.at[0, 1], plus),
        copies.start(pick(p3, 0), far.at[1, 0], minus),
    ]

    def middle():
        first[0].wait_recv()
        add_into(near.at[0], pick(p1, 0))
        second = [copies.start(near.at[0], far.at[0, 0], plus)]
        first[1].wait_recv()
        add_into(near.at[1], pick(p3, 1))
        second.append(copies.start(near.at[1], far.at[1, 1], minus))
        return second

    def last(second):
        for half, one, two in ((1, first[2], second[1]), (0, first[3], second[0])):
            one.wait_recv()
            two.wait_recv()
            own, out = pick(me, half), total.at[half]
            for i in range(leading(own)):
                at = part(own, i)
                out[at] = own[at] + far.at[0, half][at] + far.at[1, half][at]
        for copy in first + second:
            copy.wait_send()

    return middle, last


def leading(ref):
    return ref.shape[0] if len(ref.shape) == 3 else 1


def part(ref, i):
    return (i,) if len(ref.shape) == 3 else (Ellipsis,)


def add_into(out, other):
    for i in range(leading(out)):
        at = part(out, i)
        out[at] = out[at] + other[at]


def reduce_gather_kernel(
    t_ref, bias_ref, cot_ref, out_ref, g_ref, bsum_ref,
    near_a, far_a, sum_a, near_b, far_b, sum_b,
    near_c, far_c, sum_c, near_d, far_d, sum_d, pair, send, recv,
):
    here = place()
    x, z, y, h, k = here
    xp, xm = shifted(here, dx=1), shifted(here, dx=3)
    yp, ym = shifted(here, dy=1), shifted(here, dy=3)
    zp = shifted(here, dz=1)
    barrier = pltpu.get_barrier_semaphore()
    for peer in (xp, xm, yp, ym, zp):
        pl.semaphore_signal(barrier, inc=1, device_id=peer, device_id_type=MESH)
    pl.semaphore_wait(barrier, 5)
    copies = Copies(send, recv)

    mid_a, end_a = ring_sum(
        copies, lambda p, q: t_ref.at[p, q, :, 0:256, :], x, xp, xm, near_a, far_a, sum_a
    )
    mid_b, end_b = ring_sum(
        copies, lambda p, q: t_ref.at[:, q, p, 256:512, :], y, yp, ym, near_b, far_b, sum_b
    )
    second_a, second_b = mid_a(), mid_b()
    end_a(second_a)
    mid_c, end_c = ring_sum(copies, lambda p, q: sum_a.at[q, p], y, yp, ym, near_c, far_c, sum_c)
    end_b(second_b)
    mid_d, end_d = ring_sum(copies, lambda p, q: sum_b.at[q, p], x, xp, xm, near_d, far_d, sum_d)
    second_c, second_d = mid_c(), mid_d()
    other = 1 - z
    end_c(second_c)
    pair_c = copies.start(sum_c.at[other], pair.at[0], zp)
    end_d(second_d)
    pair_d = copies.start(sum_d.at[other], pair.at[1], zp)
    bias = bias_ref[...]
    lost = jnp.zeros((1, 128), F32)
    for i, (copy, total) in enumerate(((pair_c, sum_c), (pair_d, sum_d))):
        copy.wait()
        own = total[z] + pair[i]
        for b in range(2):
            pre = own[b * 128 : (b + 1) * 128].T + bias
            rows = slice((2 * i + b) * 128, (2 * i + b + 1) * 128)
            out_ref[rows] = jnp.maximum(pre, 0.0).astype(BF16)
            grad = jnp.where(pre > 0, cot_ref[rows].astype(F32), 0.0)
            lost = lost + jnp.sum(grad, axis=0, keepdims=True)
            g_ref[x, z, y, rows] = grad.astype(BF16)
    bsum_ref[...] = lost

    copies.start(g_ref.at[x, z, y], g_ref.at[x, z, y], zp).wait()
    top, low = pl.ds(0, 256), pl.ds(256, 256)
    x1, x3 = lax.rem(x + 1, 4), lax.rem(x + 3, 4)
    y1, y3 = lax.rem(y + 1, 4), lax.rem(y + 3, 4)

    def ring_gather(mine, before, after, plus, minus):
        sent = [copies.start(mine, mine, plus), copies.start(mine, mine, minus)]

        def middle():
            sent[0].wait_recv()
            sent.append(copies.start(before, before, plus))
            sent[1].wait_recv()
            sent.append(copies.start(after, after, minus))

        def last():
            sent[2].wait_recv()
            sent[3].wait_recv()
            for copy in sent:
                copy.wait_send()

        return middle, last

    mid_a, end_a = ring_gather(
        g_ref.at[x, :, y, top], g_ref.at[x, 0, y3, top], g_ref.at[x, 1, y1, top], yp, ym
    )
    mid_b, end_b = ring_gather(
        g_ref.at[x, :, y, low], g_ref.at[x3, 0, y, low], g_ref.at[x1, 1, y, low], xp, xm
    )
    mid_a()
    mid_b()
    end_a()
    mid_c, end_c = ring_gather(
        g_ref.at[x, :, :, top], g_ref.at[x3, 0, :, top], g_ref.at[x1, 1, :, top], xp, xm
    )
    end_b()
    mid_d, end_d = ring_gather(
        g_ref.at[:, :, y, low], g_ref.at[:, 0, y3, low], g_ref.at[:, 1, y1, low], yp, ym
    )
    mid_c()
    mid_d()
    end_c()
    end_d()


def reduce_gather(totals, bias, cotangent):
    vmem = pl.BlockSpec(memory_space=pltpu.VMEM)

    def ring(half):
        return [pltpu.VMEM((2,) + half, F32), pltpu.VMEM((2, 2) + half, F32), pltpu.VMEM((2,) + half, F32)]

    return pl.pallas_call(
        reduce_gather_kernel,
        out_shape=(
            jax.ShapeDtypeStruct((512, 128), BF16),
            jax.ShapeDtypeStruct((4, 2, 4, 512, 128), BF16),
            jax.ShapeDtypeStruct((1, 128), F32),
        ),
        in_specs=[vmem] * 3,
        out_specs=(vmem,) * 3,
        scratch_shapes=ring((4, 256, 128)) * 2
        + ring((256, 128)) * 2
        + [
            pltpu.VMEM((2, 256, 128), F32),
            pltpu.SemaphoreType.DMA((48,)),
            pltpu.SemaphoreType.DMA((48,)),
        ],
        compiler_params=pltpu.CompilerParams(
            collective_id=0, has_side_effects=True, vmem_limit_bytes=48 << 20
        ),
        name="reduce_gather",
    )(totals, bias, cotangent)


def finish_kernel(
    t_ref, feat_ref, weight_ref, bsum_ref, gf_ref, gw_ref,
    from_core, outgoing, from_chip, local, row_parts, total, col_parts, whole, send, recv,
):
    here = place()
    x, z, y, h, k = here
    r, c = lax.axis_index("row"), lax.axis_index("col")
    row_shifts = [(dh, dk) for dh in range(4) for dk in range(2) if (dh, dk) != (0, 0)]
    col_shifts = [
        (dx, dz, dy) for dx in range(4) for dz in range(2) for dy in range(4) if (dx, dz, dy) != (0, 0, 0)
    ]
    row_peers = [shifted(here, dh=dh, dk=dk) for dh, dk in row_shifts]
    col_peers = [shifted(here, dx=dx, dz=dz, dy=dy) for dx, dz, dy in col_shifts]
    barrier = pltpu.get_barrier_semaphore()
    for peer in row_peers + col_peers:
        pl.semaphore_signal(barrier, inc=1, device_id=peer, device_id_type=MESH)
    pl.semaphore_wait(barrier, len(row_peers) + len(col_peers))
    copies = Copies(send, recv)

    other = 1 - k
    partner = shifted(here, dk=1)
    pairs = []
    for dh in (2, 1, 3, 0):
        to = lax.rem(h + dh, 4)
        pairs.append((dh, to, copies.start(t_ref.at[to, other], from_core.at[to], partner)))
    chips = []
    for dh, to, copy in pairs[:3]:
        copy.wait_recv()
        outgoing[dh - 1] = (t_ref[to, k] + from_core[to]).astype(BF16)
        chips.append(copies.start(outgoing.at[dh - 1], from_chip.at[dh - 1], shifted(here, dh=dh)))
    pairs[3][2].wait_recv()
    own = t_ref[h, k] + from_core[h]
    for copy in chips:
        copy.wait_recv()
    for i in range(3):
        own = own + from_chip[i].astype(F32)
    grad = own.astype(BF16)
    local[0:128] = lax.dot_general(
        feat_ref[...], grad, (((0,), (0,)), ((), ())), preferred_element_type=F32
    )
    local[128:136] = jnp.concatenate([bsum_ref[...], jnp.zeros((7, 128), F32)], axis=0)
    local[136:192] = jnp.zeros((56, 128), F32)

    def piece(i):
        return local.at[pl.ds(pl.multiple_of(i * PIECE, 8), PIECE)]

    sent = [copies.start(piece(p[0]), row_parts.at[r], p) for p in row_peers]
    gf_ref[...] = lax.dot_general(
        grad, weight_ref[...], (((1,), (1,)), ((), ())), preferred_element_type=F32
    ).astype(BF16)
    row_parts[r] = piece(r)[...]
    for copy in sent:
        copy.wait_recv()
    acc = row_parts[0]
    for i in range(1, 8):
        acc = acc + row_parts[i]
    total[...] = acc
    col_parts[c] = acc
    spread = [copies.start(total, col_parts.at[c], p) for p in col_peers]
    for copy in spread:
        copy.wait_recv()
    acc = col_parts[0]
    for i in range(1, 32):
        acc = acc + col_parts[i]
    whole[r] = acc
    back = [copies.start(whole.at[r], whole.at[r], p) for p in row_peers]
    for copy in back:
        copy.wait_recv()
    for i in range(8):
        gw_ref[i] = whole[i] * (131072.0**-0.5)
    for copy in [p[2] for p in pairs] + chips + sent + spread + back:
        copy.wait_send()


def finish(partial, features, weight, bias_sum):
    vmem = pl.BlockSpec(memory_space=pltpu.VMEM)
    return pl.pallas_call(
        finish_kernel,
        out_shape=(
            jax.ShapeDtypeStruct((512, 128), BF16),
            jax.ShapeDtypeStruct((8, PIECE, 128), F32),
        ),
        in_specs=[vmem] * 4,
        out_specs=(vmem,) * 2,
        scratch_shapes=[
            pltpu.VMEM((4, 512, 128), F32),
            pltpu.VMEM((3, 512, 128), BF16),
            pltpu.VMEM((3, 512, 128), BF16),
            pltpu.VMEM((8 * PIECE, 128), F32),
            pltpu.VMEM((8, PIECE, 128), F32),
            pltpu.VMEM((PIECE, 128), F32),
            pltpu.VMEM((32, PIECE, 128), F32),
            pltpu.VMEM((8, PIECE, 128), F32),
            pltpu.SemaphoreType.DMA((56,)),
            pltpu.SemaphoreType.DMA((56,)),
        ],
        compiler_params=pltpu.CompilerParams(
            collective_id=1, has_side_effects=True, vmem_limit_bytes=32 << 20
        ),
        name="finish",
    )(partial, features, weight, bias_sum)


def shards(
    features, weight, bias, cotangent, block_count, block_rows, block_cols, edge_offsets, edge_weight
):
    count = block_count.reshape(1)
    brow, bcol = block_rows[0, 0], block_cols[0, 0]
    projected = lax.dot_general(
        weight, features.reshape(4, 128, 128), (((0,), (2,)), ((), ())), preferred_element_type=F32
    )
    projected = projected.transpose(1, 0, 2).astype(BF16)
    panel = lax.all_gather(projected, "row", axis=0, tiled=True)
    dense = densify(count, edge_offsets[0, 0], edge_weight[0, 0])
    totals = block_sums(forward_kernel, "forward", count, brow, bcol, dense, panel, 128)
    output, grads, bias_sum = reduce_gather(
        totals.reshape(4, 2, 4, 512, 128), bias.reshape(1, 128), cotangent
    )
    partial = block_sums(
        backward_kernel, "backward", count, brow, bcol, dense, grads.reshape(128, 128, 128), 32
    )
    grad_features, sums = finish(partial.reshape(4, 2, 512, 128), features, weight, bias_sum)
    sums = sums.reshape(8 * PIECE, 128)
    return (output, grad_features, sums[:128], sums[128])


def solution(mesh):
    return jax.shard_map(
        shards,
        mesh=mesh,
        in_specs=(
            P(("row", "col"), None),
            P(),
            P(),
            P(("row", "col"), None),
            P("row", "col"),
            P("row", "col", None),
            P("row", "col", None),
            P("row", "col", None, None),
            P("row", "col", None, None),
        ),
        out_specs=(P(("row", "col"), None), P(("row", "col"), None), P(), P()),
        check_vma=False,
    )
```

time: 1010 us -> 224 us (0.22)
  waiting for transfers between devices: 736 us -> 11.9 us
  blocking collectives: 185 us -> 0 us
  Pallas kernels: 0 us -> 169 us
  matrix products: 32.1 us -> 1.79 us
    reduce_scatter x2 -> x0, waiting for transfers between devices: 309 us -> none  [the longest x1 309 us: shards(): own = lax.psum_scatter(totals, 'col', scatter_dimension=0, tiled=True)]
    psum x1 -> x0, waiting for transfers between devices: 233 us -> none  [shards(): lax.psum((local_weight, local_bias), ('row', 'col'))]
    psum x1 -> x0, blocking collectives: 185 us -> none  [shards(): lax.psum((local_weight, local_bias), ('row', 'col'))]
    all_gather x2 -> x1, waiting for transfers between devices: 193 us -> 11.8 us  [shards(): panel = lax.all_gather(projected, 'row', axis=0, tiled=True)]
    pallas_call x0 -> x5, Pallas kernels: none -> 169 us  [the longest x1 91.7 us: reduce_gather(): pl.pallas_call(reduce_gather_kernel, out_shape=(jax.ShapeDtypeStruct((512...]
    dot_general x8 -> x1, matrix products: 32.1 us -> 1.79 us  [shards(): lax.dot_general(weight, features.reshape(4, 128, 128), (((0,), (2,)), (()...]
    unnamed x15 -> x28, local copies, waits for them, and re-layouts: 1.61 us -> 24.9 us
    while x2 -> x0, local copies, waits for them, and re-layouts: 15.6 us -> none  [the longest x1 11.5 us: shards(): stored, totals = lax.fori_loop(0, turns, forward_step, (stored0, totals0))]
  transfers between devices with their start and end apart: 5 -> 1, of which waited for: 4 -> 1; matrix products, arithmetic and copies ran while one was open for 0% -> 0% of each run, Pallas kernels for 0% -> 7%
where the time goes in v1:
time: 224 us
  Pallas kernels  169 us (75%)
  local copies, waits for them, and re-layouts  26 us (12%)
  between operations  14.8 us (7%)
  waiting for transfers between devices  11.9 us (5%)
    pallas_call x1, Pallas kernels, reduce_gather(): pl.pallas_call(reduce_gather_kernel, out_shape=(jax.ShapeDtypeStruct((512...  91.7 us
    pallas_call x1, Pallas kernels, finish(): pl.pallas_call(finish_kernel, out_shape=(jax.ShapeDtypeStruct((512, 128),...  48.8 us
    unnamed x28, local copies, waits for them, and re-layouts  24.9 us
    pallas_call x1, Pallas kernels, densify(): pl.pallas_call(densify_kernel, grid_spec=pltpu.PrefetchScalarGridSpec(num...  15.6 us
    pallas_call x2, Pallas kernels, block_sums(): pl.pallas_call(kernel, grid_spec=pltpu.PrefetchScalarGridSpec(num_scalar_...  13.2 us
    all_gather x1, waiting for transfers between devices, shards(): panel = lax.all_gather(projected, 'row', axis=0, tiled=True)  11.8 us
  transfers between devices with their start and end apart: 1, of which 1 were waited for; matrix products, arithmetic and copies ran while one was open for 0% of the time, Pallas kernels for 7%

profile of v1, /device:TPU:1, one launch (start us, length us, event | category | flops | bytes accessed | tf_op | source)
XLA Modules:
  0.0 223.8 jit_solution(17646865947014956747)
XLA Ops:
  7.2 0.0 all-gather.2.cloned.1.call-start
  7.2 1.8 fusion
  9.0 0.0 all-gather.2.cloned.1.call-update
  9.7 0.0 copy-start.11
  9.7 0.9 copy-done.11
  10.6 0.9 copy-done.12
  11.5 15.6 %densify.1.d_ref = bf16[512,128,128]{2,1,0:T(8,128)(2,1)S(1)} custom-call(s32[1]{0:T(128)} %bitcast.19.count_ref, s32[512,128]{1,0:T(8,128)S(1)} %bitcast.33, bf16[512,128]{1,0:T(8,128)(2,1)S(1)} %bitcast.34), custom_call_target="tpu_custom_call" | custom-call | flops 17179869184 | bytes 17170432 | tf_op jit(solution)/shard_map/densify/pallas_call | solution.py:60
  27.2 0.0 copy-start
  27.2 5.7 %copy-done = bf16[512,128,128]{2,1,0:T(8,128)(2,1)} copy-done((bf16[512,128,128]{2,1,0:T(8,128)(2,1)}, bf16[512,128,128]{2,1,0:T(8,128)(2,1)S(1)}, u32[]{:S(2)}) %copy-start) | copy-done | bytes 16777240
  32.9 11.8 %all-gather.2.cloned.1.call-done.x_ref = bf16[32,128,128]{2,1,0:T(8,128)(2,1)} async-done(((bf16[4,128,128]{2,1,0:T(8,128)(2,1)}), bf16[32,128,128]{2,1,0:T(8,128)(2,1)}) %all-gather.2.cloned.1.call-update) | async-done | bytes 1048592 | tf_op jit(solution)/shard_map/all_gather | solution.py:428
  44.8 0.0 copy-done.8
  44.8 5.8 %copy-done.1 = bf16[512,128,128]{2,1,0:T(8,128)(2,1)S(1)} copy-done((bf16[512,128,128]{2,1,0:T(8,128)(2,1)S(1)}, bf16[512,128,128]{2,1,0:T(8,128)(2,1)}, u32[]{:S(2)}) %copy-start.1) | copy-done | bytes 16777240
  50.6 1.2 copy-done.4
  51.8 6.8 %forward.1 = f32[128,128,128]{2,1,0:T(8,128)S(1)} custom-call(s32[1]{0:T(128)} %bitcast.20.count_ref, s32[512]{0:T(512)S(1)} %bitcast.28, s32[512]{0:T(512)S(1)} %bitcast.30, bf16[512,128,128]{2,1,0:T(8,128)(2,1)S(1)} %copy-done.1, bf16[32,128,128]{2,1,0:T(8,128)(2,1)S(1)} %copy-done.4), custom_call_target="tpu_custom_call" | custom-call | flops 2147483648 | bytes 16777216 | tf_op jit(solution)/shard_map/forward/pallas_call | solution.py:112
  58.6 3.2 %copy-done.3 = f32[128,128,128]{2,1,0:T(8,128)} copy-done((f32[128,128,128]{2,1,0:T(8,128)}, f32[128,128,128]{2,1,0:T(8,128)S(1)}, u32[]{:S(2)}) %copy-start.3) | copy-done | bytes 8388632
  61.8 0.0 copy-done.6
  61.9 91.7 %reduce_gather.1 = (bf16[512,128]{1,0:T(8,128)(2,1)S(1)}, bf16[4,2,4,512,128]{4,3,2,1,0:T(8,128)(2,1)S(1)}, f32[1,128]{1,0:T(1,128)S(1)}) custom-call(f32[4,2,4,512,128]{4,3,2,1,0:T(8,128)} %bitcast.22, f32[1,128]{1,0:T(1,128)S(1)} %bitcast.32, bf16[512,128]{1,0:T(8,128)(2,1)S(1)} %copy-done.6), custom_call_target="tpu_custom_call" | custom-call | tf_op jit(solution)/shard_map/reduce_gather/pallas_call | solution.py:293
  153.5 5.8 %copy-done.2 = bf16[512,128,128]{2,1,0:T(8,128)(2,1)S(1)} copy-done((bf16[512,128,128]{2,1,0:T(8,128)(2,1)S(1)}, bf16[512,128,128]{2,1,0:T(8,128)(2,1)}, u32[]{:S(2)}) %copy-start.2) | copy-done | bytes 16777240
  159.3 6.3 %backward.1 = f32[32,128,128]{2,1,0:T(8,128)S(1)} custom-call(s32[1]{0:T(128)} %bitcast.21.count_ref, s32[512]{0:T(512)S(1)} %bitcast.29, s32[512]{0:T(512)S(1)} %bitcast.31, bf16[512,128,128]{2,1,0:T(8,128)(2,1)S(1)} %copy-done.2, bf16[128,128,128]{2,1,0:T(8,128)(2,1)S(1)} %bitcast.24), custom_call_target="tpu_custom_call" | custom-call | flops 2147483648 | bytes 16777216 | tf_op jit(solution)/shard_map/backward/pallas_call | solution.py:112
  165.7 48.8 %finish.1 = (bf16[512,128]{1,0:T(8,128)(2,1)S(1)}, f32[8,24,128]{2,1,0:T(8,128)S(1)}) custom-call(f32[4,2,512,128]{3,2,1,0:T(8,128)S(1)} %bitcast.23, bf16[512,128]{1,0:T(8,128)(2,1)S(1)} %copy-done.5, bf16[128,128]{1,0:T(8,128)(2,1)S(1)} %copy-done.7, f32[1,128]{1,0:T(1,128)S(1)} %get-tuple-element.11.bsum_ref), custom_call_target="tpu_custom_call" | custom-call | tf_op jit(solution)/shard_map/finish/pallas_call | solution.py:392
  214.5 0.5 slice_bitcast_fusion
  215.0 0.6 slice.8
  215.7 0.7 copy.16
  216.3 0.7 copy.17
  (15 shorter events, 0.0 us)
Async XLA Ops:
  7.2 37.6 %all-gather.2.cloned.1.call-start = ((), (), s32[]{:S(2)}) async-start(), calls=%async_computation | async-start | bytes 1179648 | tf_op jit(solution)/shard_map/all_gather | solution.py:428
  9.7 1.0 copy-start.11
  10.6 0.9 copy-start.12
  11.5 33.2 %copy-start.8 = (s32[1,1,512]{2,1,0:T(1,128)S(1)}, s32[1,1,512]{2,1,0:T(1,128)}, u32[]{:S(2)}) copy-start(s32[1,1,512]{2,1,0:T(1,128)} %param.14) | copy-start | bytes 6148
  11.5 33.2 %copy-start.9 = (s32[1,1,512]{2,1,0:T(1,128)S(1)}, s32[1,1,512]{2,1,0:T(1,128)}, u32[]{:S(2)}) copy-start(s32[1,1,512]{2,1,0:T(1,128)} %param.15) | copy-start | bytes 6148
  27.2 5.7 %copy-start = (bf16[512,128,128]{2,1,0:T(8,128)(2,1)}, bf16[512,128,128]{2,1,0:T(8,128)(2,1)S(1)}, u32[]{:S(2)}) copy-start(bf16[512,128,128]{2,1,0:T(8,128)(2,1)S(1)} %densify.1.d_ref) | copy-start | bytes 50331652
  44.8 5.8 %copy-start.1 = (bf16[512,128,128]{2,1,0:T(8,128)(2,1)S(1)}, bf16[512,128,128]{2,1,0:T(8,128)(2,1)}, u32[]{:S(2)}) copy-start(bf16[512,128,128]{2,1,0:T(8,128)(2,1)} %copy-done) | copy-start | bytes 50331652
  50.5 1.2 copy-start.4
  51.8 10.1 %copy-start.6 = (bf16[512,128]{1,0:T(8,128)(2,1)S(1)}, bf16[512,128]{1,0:T(8,128)(2,1)}, u32[]{:S(2)}) copy-start(bf16[512,128]{1,0:T(8,128)(2,1)} %cot_ref.1) | copy-start | bytes 393220
  51.8 10.1 %copy-start.10 = (f32[128]{0:T(128)S(1)}, f32[128]{0:T(128)}, u32[]{:S(2)}) copy-start(f32[128]{0:T(128)} %param.11) | copy-start | bytes 1540
  58.6 3.2 %copy-start.3 = (f32[128,128,128]{2,1,0:T(8,128)}, f32[128,128,128]{2,1,0:T(8,128)S(1)}, u32[]{:S(2)}) copy-start(f32[128,128,128]{2,1,0:T(8,128)S(1)} %forward.1) | copy-start | bytes 25165828
  153.5 5.8 %copy-start.2 = (bf16[512,128,128]{2,1,0:T(8,128)(2,1)S(1)}, bf16[512,128,128]{2,1,0:T(8,128)(2,1)}, u32[]{:S(2)}) copy-start(bf16[512,128,128]{2,1,0:T(8,128)(2,1)} %copy-done) | copy-start | bytes 50331652
  159.3 6.4 %copy-start.5 = (bf16[512,128]{1,0:T(8,128)(2,1)S(1)}, bf16[512,128]{1,0:T(8,128)(2,1)}, u32[]{:S(2)}) copy-start(bf16[512,128]{1,0:T(8,128)(2,1)} %feat_ref.1) | copy-start | bytes 393220
  159.3 6.4 %copy-start.7 = (bf16[128,128]{1,0:T(8,128)(2,1)S(1)}, bf16[128,128]{1,0:T(8,128)(2,1)}, u32[]{:S(2)}) copy-start(bf16[128,128]{1,0:T(8,128)(2,1)} %weight_ref.1) | copy-start | bytes 98308
Sparse Core Ops, SparseCore 0:
  10.4 34.2 all-gather.1

commit v2 on v1

--- a/solution.py
+++ b/solution.py
@@ -12,6 +12,10 @@
 BF16 = jnp.bfloat16
 BATCH = 16
 PIECE = 24
+PREP_VMEM = 4 << 20
+SUMS_VMEM = 4 << 20
+REDUCE_VMEM = 16 << 20
+FINISH_VMEM = 12 << 20
 
 
 def place():
@@ -25,108 +29,6 @@
     x, z, y = lax.rem(x + dx, 4), lax.rem(z + dz, 2), lax.rem(y + dy, 4)
     h, k = lax.rem(h + dh, 4), lax.rem(k + dk, 2)
     return (h * 2 + k, x * 8 + z * 4 + y)
-
-
-def densify_kernel(count_ref, off_ref, w_ref, d_ref):
-    start = pl.program_id(0) * BATCH
-    off = off_ref[...]
-    hi = lax.shift_right_logical(off, 7).astype(F32)
-    lo = lax.bitwise_and(off, 127).astype(F32)
-    slot = start + lax.broadcasted_iota(jnp.int32, off.shape, 0)
-    w = jnp.where(slot < count_ref[0], w_ref[...].astype(F32), 0.0)
-    ids = (
-        lax.broadcasted_iota(jnp.int32, (8, 16, 128), 0) * 16
-        + lax.broadcasted_iota(jnp.int32, (8, 16, 128), 1)
-    ).astype(F32).astype(BF16)
-    one = jnp.ones((8, 16, 128), BF16)
-    zero = jnp.zeros((8, 16, 128), BF16)
-
-    def row(a, s):
-        return jnp.broadcast_to(a[s : s + 1], (16, 128)).astype(BF16)[None]
-
-    for s in range(BATCH):
-        left = jnp.where(ids == row(hi, s), jnp.broadcast_to(row(w, s), (8, 16, 128)), zero)
-        right = jnp.where(ids == row(lo, s), one, zero)
-        d_ref[s] = lax.dot_general(
-            right.reshape(128, 128),
-            left.reshape(128, 128),
-            (((1,), (1,)), ((), ())),
-            preferred_element_type=F32,
-        ).astype(BF16)
-
-
-def densify(count, offsets, weights):
-    slots = offsets.shape[0]
-    return pl.pallas_call(
-        densify_kernel,
-        grid_spec=pltpu.PrefetchScalarGridSpec(
-            num_scalar_prefetch=1,
-            grid=(slots // BATCH,),
-            in_specs=[
-                pl.BlockSpec((BATCH, 128), lambda i, n: (i, 0)),
-                pl.BlockSpec((BATCH, 128), lambda i, n: (i, 0)),
-            ],
-            out_specs=pl.BlockSpec((BATCH, 128, 128), lambda i, n: (i, 0, 0)),
-        ),
-        out_shape=jax.ShapeDtypeStruct((slots, 128, 128), BF16),
-        compiler_params=pltpu.CompilerParams(vmem_limit_bytes=16 << 20),
-        cost_estimate=pl.CostEstimate(
-            flops=slots * 128**3 * 2 * 8, bytes_accessed=slots * 128 * 262, transcendentals=0
-        ),
-        name="densify",
-    )(count, offsets, weights)
-
-
-def forward_kernel(count_ref, row_ref, col_ref, d_ref, x_ref, t_ref):
-    step = pl.program_id(0)
-
-    @pl.when(step == 0)
-    def _():
-        t_ref[...] = jnp.zeros_like(t_ref)
-
-    @pl.when(step * BATCH < count_ref[0])
-    def _():
-        for s in range(BATCH):
-            r = row_ref[step * BATCH + s]
-            c = col_ref[step * BATCH + s]
-            t_ref[r] += jnp.dot(x_ref[c], d_ref[s], preferred_element_type=F32)
-
-
-def backward_kernel(count_ref, row_ref, col_ref, d_ref, y_ref, t_ref):
-    step = pl.program_id(0)
-
-    @pl.when(step == 0)
-    def _():
-        t_ref[...] = jnp.zeros_like(t_ref)
-
-    @pl.when(step * BATCH < count_ref[0])
-    def _():
-        for s in range(BATCH):
-            r = row_ref[step * BATCH + s]
-            c = col_ref[step * BATCH + s]
-            t_ref[c] += jnp.dot(d_ref[s], y_ref[r], preferred_element_type=F32)
-
-
-def block_sums(kernel, name, count, brow, bcol, dense, panel, blocks):
-    slots = dense.shape[0]
-    return pl.pallas_call(
-        kernel,
-        grid_spec=pltpu.PrefetchScalarGridSpec(
-            num_scalar_prefetch=3,
-            grid=(slots // BATCH,),
-            in_specs=[
-                pl.BlockSpec((BATCH, 128, 128), lambda i, *_: (i, 0, 0)),
-                pl.BlockSpec(memory_space=pltpu.VMEM),
-            ],
-            out_specs=pl.BlockSpec(memory_space=pltpu.VMEM),
-        ),
-        out_shape=jax.ShapeDtypeStruct((blocks, 128, 128), F32),
-        compiler_params=pltpu.CompilerParams(vmem_limit_bytes=24 << 20),
-        cost_estimate=pl.CostEstimate(
-            flops=slots * 128**3 * 2, bytes_accessed=slots * 128 * 256, transcendentals=0
-        ),
-        name=name,
-    )(count, brow, bcol, dense, panel)
 
 
 class Copies:
@@ -145,6 +47,124 @@
         self.used += 1
         copy.start()
         return copy
+
+
+def prepare_kernel(count_ref, off_ref, w_ref, feat_ref, weight_ref, d_ref, panel_ref, send, recv):
+    here = place()
+    x, z, y, h, k = here
+    r = lax.axis_index("row")
+    partner = shifted(here, dk=1)
+    chips = [shifted(here, dh=dh) for dh in (2, 1, 3)]
+    barrier = pltpu.get_barrier_semaphore()
+    for peer in [partner] + chips:
+        pl.semaphore_signal(barrier, inc=1, device_id=peer, device_id_type=MESH)
+    for b in range(4):
+        rows = slice(b * 128, (b + 1) * 128)
+        projected = jnp.dot(feat_ref[rows], weight_ref[...], preferred_element_type=F32)
+        panel_ref[r, b] = projected.T.astype(BF16)
+    pl.semaphore_wait(barrier, 4)
+    copies = Copies(send, recv)
+    away = [copies.start(panel_ref.at[r], panel_ref.at[r], p) for p in chips]
+    beside = [copies.start(panel_ref.at[r], panel_ref.at[r], partner)]
+
+    count = count_ref[0, 0]
+    ids = (
+        lax.broadcasted_iota(jnp.int32, (8, 16, 128), 0) * 16
+        + lax.broadcasted_iota(jnp.int32, (8, 16, 128), 1)
+    ).astype(F32).astype(BF16)
+    one = jnp.ones((8, 16, 128), BF16)
+    zero = jnp.zeros((8, 16, 128), BF16)
+
+    def row(a, s):
+        return jnp.broadcast_to(a[s : s + 1], (16, 128)).astype(BF16)[None]
+
+    def densify(step, carry):
+        start = pl.multiple_of(step * BATCH, BATCH)
+        off = off_ref[pl.ds(start, BATCH)]
+        hi = lax.shift_right_logical(off, 7).astype(F32)
+        lo = lax.bitwise_and(off, 127).astype(F32)
+        slot = start + lax.broadcasted_iota(jnp.int32, off.shape, 0)
+        w = jnp.where(slot < count, w_ref[pl.ds(start, BATCH)].astype(F32), 0.0)
+        for s in range(BATCH):
+            left = jnp.where(ids == row(hi, s), jnp.broadcast_to(row(w, s), (8, 16, 128)), zero)
+            right = jnp.where(ids == row(lo, s), one, zero)
+            d_ref[start + s] = lax.dot_general(
+                right.reshape(128, 128),
+                left.reshape(128, 128),
+                (((1,), (1,)), ((), ())),
+                preferred_element_type=F32,
+            ).astype(BF16)
+        return carry
+
+    steps = d_ref.shape[0] // BATCH
+    lax.fori_loop(0, steps * 3 // 4, densify, 0)
+    for dh, copy in zip((2, 1, 3), away):
+        copy.wait_recv()
+        got = panel_ref.at[lax.rem(h - dh + 4, 4) * 2 + k]
+        beside.append(copies.start(got, got, partner))
+    lax.fori_loop(steps * 3 // 4, steps, densify, 0)
+    for copy in beside:
+        copy.wait_recv()
+    for copy in away + beside:
+        copy.wait_send()
+
+
+def prepare(count, offsets, weights, features, weight):
+    slots = offsets.shape[0]
+    vmem = pl.BlockSpec(memory_space=pltpu.VMEM)
+    return pl.pallas_call(
+        prepare_kernel,
+        out_shape=(
+            jax.ShapeDtypeStruct((slots, 128, 128), BF16),
+            jax.ShapeDtypeStruct((8, 4, 128, 128), BF16),
+        ),
+        in_specs=[pl.BlockSpec(memory_space=pltpu.SMEM)] + [vmem] * 4,
+        out_specs=(vmem,) * 2,
+        scratch_shapes=[pltpu.SemaphoreType.DMA((7,)), pltpu.SemaphoreType.DMA((7,))],
+        compiler_params=pltpu.CompilerParams(
+            collective_id=2, has_side_effects=True, vmem_limit_bytes=PREP_VMEM
+        ),
+        name="prepare",
+    )(count, offsets, weights, features, weight)
+
+
+def forward_kernel(count_ref, row_ref, col_ref, d_ref, x_ref, t_ref):
+    t_ref[...] = jnp.zeros_like(t_ref)
+
+    def step(i, carry):
+        for s in range(BATCH):
+            n = i * BATCH + s
+            r, c = row_ref[n], col_ref[n]
+            t_ref[r] += jnp.dot(x_ref[c], d_ref[n], preferred_element_type=F32)
+        return carry
+
+    lax.fori_loop(0, lax.div(count_ref[0, 0] + (BATCH - 1), BATCH), step, 0)
+
+
+def backward_kernel(count_ref, row_ref, col_ref, d_ref, y_ref, t_ref):
+    t_ref[...] = jnp.zeros_like(t_ref)
+
+    def step(i, carry):
+        for s in range(BATCH):
+            n = i * BATCH + s
+            r, c = row_ref[n], col_ref[n]
+            t_ref[c] += jnp.dot(d_ref[n], y_ref[r], preferred_element_type=F32)
+        return carry
+
+    lax.fori_loop(0, lax.div(count_ref[0, 0] + (BATCH - 1), BATCH), step, 0)
+
+
+def block_sums(kernel, name, count, brow, bcol, dense, panel, blocks):
+    slots = dense.shape[0]
+    smem, vmem = pl.BlockSpec(memory_space=pltpu.SMEM), pl.BlockSpec(memory_space=pltpu.VMEM)
+    return pl.pallas_call(
+        kernel,
+        in_specs=[smem] * 3 + [vmem] * 2,
+        out_specs=vmem,
+        out_shape=jax.ShapeDtypeStruct((blocks, 128, 128), F32),
+        compiler_params=pltpu.CompilerParams(vmem_limit_bytes=SUMS_VMEM),
+        name=name,
+    )(count, brow, bcol, dense, panel)
 
 
 def ring_sum(copies, pick, me, plus, minus, near, far, total):
@@ -307,14 +327,14 @@
             pltpu.SemaphoreType.DMA((48,)),
         ],
         compiler_params=pltpu.CompilerParams(
-            collective_id=0, has_side_effects=True, vmem_limit_bytes=48 << 20
+            collective_id=0, has_side_effects=True, vmem_limit_bytes=REDUCE_VMEM
         ),
         name="reduce_gather",
     )(totals, bias, cotangent)
 
 
 def finish_kernel(
-    t_ref, feat_ref, weight_ref, bsum_ref, gf_ref, gw_ref,
+    t_ref, feat_ref, weight_ref, bsum_ref, gf_ref, gw_ref, gb_ref,
     from_core, outgoing, from_chip, local, row_parts, total, col_parts, whole, send, recv,
 ):
     here = place()
@@ -377,12 +397,14 @@
     acc = col_parts[0]
     for i in range(1, 32):
         acc = acc + col_parts[i]
-    whole[r] = acc
-    back = [copies.start(whole.at[r], whole.at[r], p) for p in row_peers]
+    mine = whole.at[pl.ds(pl.multiple_of(r * PIECE, 8), PIECE)]
+    mine[...] = acc
+    back = [copies.start(mine, mine, p) for p in row_peers]
     for copy in back:
         copy.wait_recv()
-    for i in range(8):
-        gw_ref[i] = whole[i] * (131072.0**-0.5)
+    scale = 131072.0**-0.5
+    gw_ref[...] = whole[0:128] * scale
+    gb_ref[...] = whole[128:129] * scale
     for copy in [p[2] for p in pairs] + chips + sent + spread + back:
         copy.wait_send()
 
@@ -393,10 +415,11 @@
         finish_kernel,
         out_shape=(
             jax.ShapeDtypeStruct((512, 128), BF16),
-            jax.ShapeDtypeStruct((8, PIECE, 128), F32),
+            jax.ShapeDtypeStruct((128, 128), F32),
+            jax.ShapeDtypeStruct((1, 128), F32),
         ),
         in_specs=[vmem] * 4,
-        out_specs=(vmem,) * 2,
+        out_specs=(vmem,) * 3,
         scratch_shapes=[
             pltpu.VMEM((4, 512, 128), F32),
             pltpu.VMEM((3, 512, 128), BF16),
@@ -405,12 +428,12 @@
             pltpu.VMEM((8, PIECE, 128), F32),
             pltpu.VMEM((PIECE, 128), F32),
             pltpu.VMEM((32, PIECE, 128), F32),
-            pltpu.VMEM((8, PIECE, 128), F32),
+            pltpu.VMEM((8 * PIECE, 128), F32),
             pltpu.SemaphoreType.DMA((56,)),
             pltpu.SemaphoreType.DMA((56,)),
         ],
         compiler_params=pltpu.CompilerParams(
-            collective_id=1, has_side_effects=True, vmem_limit_bytes=32 << 20
+            collective_id=1, has_side_effects=True, vmem_limit_bytes=FINISH_VMEM
         ),
         name="finish",
     )(partial, features, weight, bias_sum)
@@ -419,24 +442,21 @@
 def shards(
     features, weight, bias, cotangent, block_count, block_rows, block_cols, edge_offsets, edge_weight
 ):
-    count = block_count.reshape(1)
     brow, bcol = block_rows[0, 0], block_cols[0, 0]
-    projected = lax.dot_general(
-        weight, features.reshape(4, 128, 128), (((0,), (2,)), ((), ())), preferred_element_type=F32
-    )
-    projected = projected.transpose(1, 0, 2).astype(BF16)
-    panel = lax.all_gather(projected, "row", axis=0, tiled=True)
-    dense = densify(count, edge_offsets[0, 0], edge_weight[0, 0])
-    totals = block_sums(forward_kernel, "forward", count, brow, bcol, dense, panel, 128)
+    dense, panel = prepare(block_count, edge_offsets[0, 0], edge_weight[0, 0], features, weight)
+    totals = block_sums(
+        forward_kernel, "forward", block_count, brow, bcol, dense, panel.reshape(32, 128, 128), 128
+    )
     output, grads, bias_sum = reduce_gather(
         totals.reshape(4, 2, 4, 512, 128), bias.reshape(1, 128), cotangent
     )
     partial = block_sums(
-        backward_kernel, "backward", count, brow, bcol, dense, grads.reshape(128, 128, 128), 32
-    )
-    grad_features, sums = finish(partial.reshape(4, 2, 512, 128), features, weight, bias_sum)
-    sums = sums.reshape(8 * PIECE, 128)
-    return (output, grad_features, sums[:128], sums[128])
+        backward_kernel, "backward", block_count, brow, bcol, dense, grads.reshape(128, 128, 128), 32
+    )
+    grad_features, grad_weight, grad_bias = finish(
+        partial.reshape(4, 2, 512, 128), features, weight, bias_sum
+    )
+    return (output, grad_features, grad_weight, grad_bias.reshape(128))
 
 
 def solution(mesh):

time: 224 us -> 184 us (0.82)
  local copies, waits for them, and re-layouts: 26 us -> 7.33 us
  between operations: 14.8 us -> 1.37 us
  waiting for transfers between devices: 11.9 us -> 0 us
  Pallas kernels: 169 us -> 175 us
    unnamed x28 -> x22, local copies, waits for them, and re-layouts: 24.9 us -> 7.33 us
    all_gather x1 -> x0, waiting for transfers between devices: 11.8 us -> none  [shards(): panel = lax.all_gather(projected, 'row', axis=0, tiled=True)]
    pallas_call x1, Pallas kernels: 48.8 us -> 55.3 us  [finish(): pl.pallas_call(finish_kernel, out_shape=(jax.ShapeDtypeStruct((512, 128),...]
  transfers between devices with their start and end apart: 1 -> 0, of which waited for: 1 -> 0; matrix products, arithmetic and copies ran while one was open for 0% -> 0% of each run, Pallas kernels for 7% -> 0%
where the time goes in v2:
time: 184 us; the launch traced here: 183 us
  Pallas kernels  175 us (95%)
  local copies, waits for them, and re-layouts  7.33 us (4%)
    pallas_call x1, Pallas kernels, reduce_gather(): pl.pallas_call(reduce_gather_kernel, out_shape=(jax.ShapeDtypeStruct((512...  91 us
    pallas_call x1, Pallas kernels, finish(): pl.pallas_call(finish_kernel, out_shape=(jax.ShapeDtypeStruct((512, 128),...  55.3 us
    pallas_call x1, Pallas kernels, prepare(): pl.pallas_call(prepare_kernel, out_shape=(jax.ShapeDtypeStruct((slots, 12...  24 us
    unnamed x22, local copies, waits for them, and re-layouts  7.33 us
    pallas_call x2, Pallas kernels, block_sums(): pl.pallas_call(kernel, in_specs=[smem] * 3 + [vmem] * 2, out_specs=vmem,...  4.35 us

profile of v2, /device:TPU:1, one launch (start us, length us, event | category | flops | bytes accessed | tf_op | source)
XLA Modules:
  0.0 183.3 jit_solution(8670186595534292417)
XLA Ops:
  1.3 0.0 copy-start
  1.3 0.9 copy-done
  2.2 0.9 copy-done.2
  3.1 0.0 copy-start.4
  3.1 0.8 copy-done.4
  3.9 0.0 copy-start.5
  3.9 0.9 copy-done.5
  4.8 24.0 %prepare.1 = (bf16[512,128,128]{2,1,0:T(8,128)(2,1)S(1)}, bf16[8,4,128,128]{3,2,1,0:T(8,128)(2,1)S(1)}) custom-call(s32[1,1]{1,0:T(1,128)S(6)} %copy.17.count_ref, s32[512,128]{1,0:T(8,128)S(1)} %bitcast.14, bf16[512,128]{1,0:T(8,128)(2,1)S(1)} %bitcast.15, bf16[512,128]{1,0:T(8,128)(2,1)S(1)} %copy-done, bf16[128,128]{1,0:T(8,128)(2,1)S(1)} %copy-done.4), custom_call_target="tpu_custom_call" | custom-call | tf_op jit(solution)/shard_map/prepare/pallas_call | solution.py:115
  28.8 0.0 copy-start.6
  28.8 0.7 copy-done.6
  29.5 0.0 copy-start.7
  29.5 0.7 copy-done.7
  30.1 2.3 %forward.1 = f32[128,128,128]{2,1,0:T(8,128)S(1)} custom-call(s32[1,1]{1,0:T(1,128)S(6)} %copy.17.count_ref, s32[512]{0:T(512)S(1)} %bitcast.16, s32[512]{0:T(512)S(1)} %bitcast.18, bf16[512,128,128]{2,1,0:T(8,128)(2,1)S(1)} %get-tuple-element.12.d_ref, bf16[32,128,128]{2,1,0:T(8,128)(2,1)S(1)} %bitcast.13), custom_call_target="tpu_custom_call" | custom-call | tf_op jit(solution)/shard_map/forward/pallas_call | solution.py:160
  32.5 0.0 copy-done.3
  32.5 0.0 copy-done.8
  32.5 91.0 %reduce_gather.1 = (bf16[512,128]{1,0:T(8,128)(2,1)S(1)}, bf16[4,2,4,512,128]{4,3,2,1,0:T(8,128)(2,1)S(1)}, f32[1,128]{1,0:T(1,128)S(1)}) custom-call(f32[4,2,4,512,128]{4,3,2,1,0:T(8,128)S(1)} %bitcast.10, f32[1,128]{1,0:T(1,128)S(1)} %bitcast.20, bf16[512,128]{1,0:T(8,128)(2,1)S(1)} %copy-done.3), custom_call_target="tpu_custom_call" | custom-call | tf_op jit(solution)/shard_map/reduce_gather/pallas_call | solution.py:313
  123.5 0.0 copy-start.1
  123.5 2.0 %backward.1 = f32[32,128,128]{2,1,0:T(8,128)S(1)} custom-call(s32[1,1]{1,0:T(1,128)S(6)} %copy.17.count_ref, s32[512]{0:T(512)S(1)} %bitcast.17, s32[512]{0:T(512)S(1)} %bitcast.19, bf16[512,128,128]{2,1,0:T(8,128)(2,1)S(1)} %get-tuple-element.12.d_ref, bf16[128,128,128]{2,1,0:T(8,128)(2,1)S(1)} %bitcast.12), custom_call_target="tpu_custom_call" | custom-call | tf_op jit(solution)/shard_map/backward/pallas_call | solution.py:160
  125.5 0.0 copy-done.1
  125.5 55.3 %finish.1 = (bf16[512,128]{1,0:T(8,128)(2,1)S(1)}, f32[128,128]{1,0:T(8,128)S(1)}, f32[1,128]{1,0:T(1,128)S(1)}) custom-call(f32[4,2,512,128]{3,2,1,0:T(8,128)S(1)} %bitcast.11, bf16[512,128]{1,0:T(8,128)(2,1)S(1)} %copy-done.1, bf16[128,128]{1,0:T(8,128)(2,1)S(1)} %copy-done.4, f32[1,128]{1,0:T(1,128)S(1)} %get-tuple-element.16.bsum_ref), custom_call_target="tpu_custom_call" | custom-call | tf_op jit(solution)/shard_map/finish/pallas_call | solution.py:414
  180.8 0.7 copy.18
  181.5 0.7 copy.19
  182.2 0.6 copy.20
  182.8 0.5 copy.21
  (3 shorter events, 0.0 us)
Async XLA Ops:
  1.3 0.9 copy-start
  2.2 0.9 copy-start.2
  3.1 0.8 copy-start.4
  3.9 0.9 copy-start.5
  28.8 0.7 copy-start.6
  29.5 0.7 copy-start.7
  30.1 2.4 %copy-start.3 = (bf16[512,128]{1,0:T(8,128)(2,1)S(1)}, bf16[512,128]{1,0:T(8,128)(2,1)}, u32[]{:S(2)}) copy-start(bf16[512,128]{1,0:T(8,128)(2,1)} %cot_ref.1) | copy-start | bytes 393220
  30.1 2.4 %copy-start.8 = (f32[128]{0:T(128)S(1)}, f32[128]{0:T(128)}, u32[]{:S(2)}) copy-start(f32[128]{0:T(128)} %param.11) | copy-start | bytes 1540
  123.5 2.0 %copy-start.1 = (bf16[512,128]{1,0:T(8,128)(2,1)S(1)}, bf16[512,128]{1,0:T(8,128)(2,1)}, u32[]{:S(2)}) copy-start(bf16[512,128]{1,0:T(8,128)(2,1)} %feat_ref.3) | copy-start | bytes 393220

commit v3 on v2

--- a/solution.py
+++ b/solution.py
@@ -167,56 +167,80 @@
     )(count, brow, bcol, dense, panel)
 
 
-def ring_sum(copies, pick, me, plus, minus, near, far, total):
+LEVELS = 32766.0
+
+
+def blocks_of(ref):
+    if len(ref.shape) == 2:
+        return [(pl.ds(128 * b, 128),) for b in range(2)]
+    return [(i, pl.ds(128 * b, 128)) for i in range(ref.shape[0]) for b in range(2)]
+
+
+def encode(value, at, n, q_ref, s_ref):
+    size = jnp.abs(value)
+    most = jnp.maximum(jnp.max(size, axis=0, keepdims=True), 1e-30)
+    level = jnp.sqrt(size * (1.0 / most)) * LEVELS + 0.5
+    q_ref[at] = jnp.where(value < 0, -level, level).astype(jnp.int32).astype(jnp.int16)
+    s_ref[n : n + 1] = most * (1.0 / (LEVELS * LEVELS))
+
+
+def decode(at, n, q_ref, s_ref):
+    level = q_ref[at].astype(jnp.int32).astype(F32)
+    return level * jnp.abs(level) * s_ref[n : n + 1]
+
+
+def ring_sum(copies, pick, me, plus, minus, q, scales, total):
     p1, p2, p3 = lax.rem(me + 1, 4), lax.rem(me + 2, 4), lax.rem(me + 3, 4)
+
+    def send(value, slot, device):
+        for n, at in enumerate(blocks_of(q.at[slot])):
+            encode(value(n, at), at, n, q.at[slot], scales.at[slot])
+        return (
+            copies.start(q.at[slot], q.at[slot + 6], device),
+            copies.start(scales.at[slot], scales.at[slot + 6], device),
+        )
+
+    def got(slot):
+        return lambda n, at: decode(at, n, q.at[slot + 6], scales.at[slot + 6])
+
+    def own(p, half):
+        return lambda n, at: pick(p, half)[at]
+
+    def plus_got(p, half, slot):
+        return lambda n, at: own(p, half)(n, at) + got(slot)(n, at)
+
     first = [
-        copies.start(pick(p2, 0), near.at[0], plus),
-        copies.start(pick(p2, 1), near.at[1], minus),
-        copies.start(pick(p1, 1), far.at[0, 1], plus),
-        copies.start(pick(p3, 0), far.at[1, 0], minus),
+        send(own(p2, 0), 0, plus),
+        send(own(p2, 1), 1, minus),
+        send(own(p1, 1), 2, plus),
+        send(own(p3, 0), 3, minus),
     ]
 
     def middle():
-        first[0].wait_recv()
-        add_into(near.at[0], pick(p1, 0))
-        second = [copies.start(near.at[0], far.at[0, 0], plus)]
-        first[1].wait_recv()
-        add_into(near.at[1], pick(p3, 1))
-        second.append(copies.start(near.at[1], far.at[1, 1], minus))
+        second = []
+        for slot, p, half, device in ((0, p1, 0, plus), (1, p3, 1, minus)):
+            for copy in first[slot]:
+                copy.wait_recv()
+            second.append(send(plus_got(p, half, slot), slot + 4, device))
         return second
 
     def last(second):
-        for half, one, two in ((1, first[2], second[1]), (0, first[3], second[0])):
-            one.wait_recv()
-            two.wait_recv()
-            own, out = pick(me, half), total.at[half]
-            for i in range(leading(own)):
-                at = part(own, i)
-                out[at] = own[at] + far.at[0, half][at] + far.at[1, half][at]
-        for copy in first + second:
-            copy.wait_send()
+        for half, one, two in ((1, 2, 5), (0, 3, 4)):
+            for copy in first[one] + second[two - 4]:
+                copy.wait_recv()
+            out = total.at[half]
+            for n, at in enumerate(blocks_of(out)):
+                out[at] = own(me, half)(n, at) + got(one)(n, at) + got(two)(n, at)
+        for pair in first + second:
+            for copy in pair:
+                copy.wait_send()
 
     return middle, last
-
-
-def leading(ref):
-    return ref.shape[0] if len(ref.shape) == 3 else 1
-
-
-def part(ref, i):
-    return (i,) if len(ref.shape) == 3 else (Ellipsis,)
-
-
-def add_into(out, other):
-    for i in range(leading(out)):
-        at = part(out, i)
-        out[at] = out[at] + other[at]
 
 
 def reduce_gather_kernel(
     t_ref, bias_ref, cot_ref, out_ref, g_ref, bsum_ref,
-    near_a, far_a, sum_a, near_b, far_b, sum_b,
-    near_c, far_c, sum_c, near_d, far_d, sum_d, pair, send, recv,
+    q_a, scale_a, sum_a, q_b, scale_b, sum_b, q_c, scale_c, sum_c, q_d, scale_d, sum_d, pair, send, recv,
 ):
     here = place()
     x, z, y, h, k = here
@@ -230,16 +254,16 @@
     copies = Copies(send, recv)
 
     mid_a, end_a = ring_sum(
-        copies, lambda p, q: t_ref.at[p, q, :, 0:256, :], x, xp, xm, near_a, far_a, sum_a
+        copies, lambda p, q: t_ref.at[p, q, :, 0:256, :], x, xp, xm, q_a, scale_a, sum_a
     )
     mid_b, end_b = ring_sum(
-        copies, lambda p, q: t_ref.at[:, q, p, 256:512, :], y, yp, ym, near_b, far_b, sum_b
+        copies, lambda p, q: t_ref.at[:, q, p, 256:512, :], y, yp, ym, q_b, scale_b, sum_b
     )
     second_a, second_b = mid_a(), mid_b()
     end_a(second_a)
-    mid_c, end_c = ring_sum(copies, lambda p, q: sum_a.at[q, p], y, yp, ym, near_c, far_c, sum_c)
+    mid_c, end_c = ring_sum(copies, lambda p, q: sum_a.at[q, p], y, yp, ym, q_c, scale_c, sum_c)
     end_b(second_b)
-    mid_d, end_d = ring_sum(copies, lambda p, q: sum_b.at[q, p], x, xp, xm, near_d, far_d, sum_d)
+    mid_d, end_d = ring_sum(copies, lambda p, q: sum_b.at[q, p], x, xp, xm, q_d, scale_d, sum_d)
     second_c, second_d = mid_c(), mid_d()
     other = 1 - z
     end_c(second_c)
@@ -308,7 +332,11 @@
     vmem = pl.BlockSpec(memory_space=pltpu.VMEM)
 
     def ring(half):
-        return [pltpu.VMEM((2,) + half, F32), pltpu.VMEM((2, 2) + half, F32), pltpu.VMEM((2,) + half, F32)]
+        return [
+            pltpu.VMEM((12,) + half, jnp.int16),
+            pltpu.VMEM((12, 8, 128), F32),
+            pltpu.VMEM((2,) + half, F32),
+        ]
 
     return pl.pallas_call(
         reduce_gather_kernel,
@@ -323,8 +351,8 @@
         + ring((256, 128)) * 2
         + [
             pltpu.VMEM((2, 256, 128), F32),
-            pltpu.SemaphoreType.DMA((48,)),
-            pltpu.SemaphoreType.DMA((48,)),
+            pltpu.SemaphoreType.DMA((72,)),
+            pltpu.SemaphoreType.DMA((72,)),
         ],
         compiler_params=pltpu.CompilerParams(
             collective_id=0, has_side_effects=True, vmem_limit_bytes=REDUCE_VMEM

time: 184 us -> 166 us (0.902)
  Pallas kernels: 175 us -> 157 us
    pallas_call x1, Pallas kernels: 91 us -> 73.3 us  [reduce_gather(): pl.pallas_call(reduce_gather_kernel, out_shape=(jax.ShapeDtypeStruct((512...]
    pallas_call x1, Pallas kernels: 55.3 us -> 52.5 us  [finish(): pl.pallas_call(finish_kernel, out_shape=(jax.ShapeDtypeStruct((512, 128),...]
    pallas_call x2, Pallas kernels: 4.35 us -> 6.85 us  [block_sums(): pl.pallas_call(kernel, in_specs=[smem] * 3 + [vmem] * 2, out_specs=vmem,...]
where the time goes in v3:
time: 166 us; the launch traced here: 165 us
  Pallas kernels  157 us (95%)
  local copies, waits for them, and re-layouts  7.33 us (4%)
    pallas_call x1, Pallas kernels, reduce_gather(): pl.pallas_call(reduce_gather_kernel, out_shape=(jax.ShapeDtypeStruct((512...  73.3 us
    pallas_call x1, Pallas kernels, finish(): pl.pallas_call(finish_kernel, out_shape=(jax.ShapeDtypeStruct((512, 128),...  52.5 us
    pallas_call x1, Pallas kernels, prepare(): pl.pallas_call(prepare_kernel, out_shape=(jax.ShapeDtypeStruct((slots, 12...  24 us
    unnamed x22, local copies, waits for them, and re-layouts  7.33 us
    pallas_call x2, Pallas kernels, block_sums(): pl.pallas_call(kernel, in_specs=[smem] * 3 + [vmem] * 2, out_specs=vmem,...  6.85 us

profile of v3, /device:TPU:1, one launch (start us, length us, event | category | flops | bytes accessed | tf_op | source)
XLA Modules:
  0.0 165.3 jit_solution(17623355205035052395)
XLA Ops:
  1.3 0.0 copy-start
  1.3 0.9 copy-done
  2.2 0.9 copy-done.2
  3.1 0.0 copy-start.4
  3.1 0.8 copy-done.4
  3.9 0.0 copy-start.5
  3.9 0.9 copy-done.5
  4.8 24.0 %prepare.1 = (bf16[512,128,128]{2,1,0:T(8,128)(2,1)S(1)}, bf16[8,4,128,128]{3,2,1,0:T(8,128)(2,1)S(1)}) custom-call(s32[1,1]{1,0:T(1,128)S(6)} %copy.17.count_ref, s32[512,128]{1,0:T(8,128)S(1)} %bitcast.14, bf16[512,128]{1,0:T(8,128)(2,1)S(1)} %bitcast.15, bf16[512,128]{1,0:T(8,128)(2,1)S(1)} %copy-done, bf16[128,128]{1,0:T(8,128)(2,1)S(1)} %copy-done.4), custom_call_target="tpu_custom_call" | custom-call | tf_op jit(solution)/shard_map/prepare/pallas_call | solution.py:115
  28.8 0.0 copy-start.6
  28.8 0.7 copy-done.6
  29.5 0.0 copy-start.7
  29.5 0.7 copy-done.7
  30.1 3.6 %forward.1 = f32[128,128,128]{2,1,0:T(8,128)S(1)} custom-call(s32[1,1]{1,0:T(1,128)S(6)} %copy.17.count_ref, s32[512]{0:T(512)S(1)} %bitcast.16, s32[512]{0:T(512)S(1)} %bitcast.18, bf16[512,128,128]{2,1,0:T(8,128)(2,1)S(1)} %get-tuple-element.12.d_ref, bf16[32,128,128]{2,1,0:T(8,128)(2,1)S(1)} %bitcast.13), custom_call_target="tpu_custom_call" | custom-call | tf_op jit(solution)/shard_map/forward/pallas_call | solution.py:160
  33.7 0.0 copy-done.3
  33.7 0.0 copy-done.8
  33.7 73.3 %reduce_gather.1 = (bf16[512,128]{1,0:T(8,128)(2,1)S(1)}, bf16[4,2,4,512,128]{4,3,2,1,0:T(8,128)(2,1)S(1)}, f32[1,128]{1,0:T(1,128)S(1)}) custom-call(f32[4,2,4,512,128]{4,3,2,1,0:T(8,128)S(1)} %bitcast.10, f32[1,128]{1,0:T(1,128)S(1)} %bitcast.20, bf16[512,128]{1,0:T(8,128)(2,1)S(1)} %copy-done.3), custom_call_target="tpu_custom_call" | custom-call | tf_op jit(solution)/shard_map/reduce_gather/pallas_call | solution.py:341
  107.0 0.0 copy-start.1
  107.0 3.3 %backward.1 = f32[32,128,128]{2,1,0:T(8,128)S(1)} custom-call(s32[1,1]{1,0:T(1,128)S(6)} %copy.17.count_ref, s32[512]{0:T(512)S(1)} %bitcast.17, s32[512]{0:T(512)S(1)} %bitcast.19, bf16[512,128,128]{2,1,0:T(8,128)(2,1)S(1)} %get-tuple-element.12.d_ref, bf16[128,128,128]{2,1,0:T(8,128)(2,1)S(1)} %bitcast.12), custom_call_target="tpu_custom_call" | custom-call | tf_op jit(solution)/shard_map/backward/pallas_call | solution.py:160
  110.3 0.0 copy-done.1
  110.3 52.5 %finish.1 = (bf16[512,128]{1,0:T(8,128)(2,1)S(1)}, f32[128,128]{1,0:T(8,128)S(1)}, f32[1,128]{1,0:T(1,128)S(1)}) custom-call(f32[4,2,512,128]{3,2,1,0:T(8,128)S(1)} %bitcast.11, bf16[512,128]{1,0:T(8,128)(2,1)S(1)} %copy-done.1, bf16[128,128]{1,0:T(8,128)(2,1)S(1)} %copy-done.4, f32[1,128]{1,0:T(1,128)S(1)} %get-tuple-element.16.bsum_ref), custom_call_target="tpu_custom_call" | custom-call | tf_op jit(solution)/shard_map/finish/pallas_call | solution.py:442
  162.8 0.7 copy.18
  163.5 0.7 copy.19
  164.2 0.6 copy.20
  164.8 0.5 copy.21
  (3 shorter events, 0.0 us)
Async XLA Ops:
  1.3 0.9 copy-start
  2.2 0.9 copy-start.2
  3.1 0.8 copy-start.4
  3.9 0.9 copy-start.5
  28.8 0.7 copy-start.6
  29.5 0.7 copy-start.7
  30.1 3.6 %copy-start.3 = (bf16[512,128]{1,0:T(8,128)(2,1)S(1)}, bf16[512,128]{1,0:T(8,128)(2,1)}, u32[]{:S(2)}) copy-start(bf16[512,128]{1,0:T(8,128)(2,1)} %cot_ref.1) | copy-start | bytes 393220
  30.1 3.6 %copy-start.8 = (f32[128]{0:T(128)S(1)}, f32[128]{0:T(128)}, u32[]{:S(2)}) copy-start(f32[128]{0:T(128)} %param.11) | copy-start | bytes 1540
  107.0 3.3 %copy-start.1 = (bf16[512,128]{1,0:T(8,128)(2,1)S(1)}, bf16[512,128]{1,0:T(8,128)(2,1)}, u32[]{:S(2)}) copy-start(bf16[512,128]{1,0:T(8,128)(2,1)} %feat_ref.3) | copy-start | bytes 393220

commit v4 on v3

--- a/solution.py
+++ b/solution.py
@@ -10,8 +10,7 @@
 MESH = pl.DeviceIdType.MESH
 F32 = jnp.float32
 BF16 = jnp.bfloat16
-BATCH = 16
-PIECE = 24
+BATCH = 64
 PREP_VMEM = 4 << 20
 SUMS_VMEM = 4 << 20
 REDUCE_VMEM = 16 << 20
@@ -49,7 +48,23 @@
         return copy
 
 
-def prepare_kernel(count_ref, off_ref, w_ref, feat_ref, weight_ref, d_ref, panel_ref, send, recv):
+def prepare_kernel(
+    count_ref, off_hbm, w_hbm, feat_hbm, weight_hbm, d_ref, panel_ref,
+    off_ref, w_ref, feat_ref, weight_ref, load, send, recv,
+):
+    loads = [
+        pltpu.make_async_copy(source, target, load.at[i])
+        for i, (source, target) in enumerate(
+            (
+                (feat_hbm, feat_ref),
+                (weight_hbm, weight_ref),
+                (off_hbm.at[0, 0], off_ref),
+                (w_hbm.at[0, 0], w_ref),
+            )
+        )
+    ]
+    for copy in loads:
+        copy.start()
     here = place()
     x, z, y, h, k = here
     r = lax.axis_index("row")
@@ -58,6 +73,8 @@
     barrier = pltpu.get_barrier_semaphore()
     for peer in [partner] + chips:
         pl.semaphore_signal(barrier, inc=1, device_id=peer, device_id_type=MESH)
+    loads[0].wait()
+    loads[1].wait()
     for b in range(4):
         rows = slice(b * 128, (b + 1) * 128)
         projected = jnp.dot(feat_ref[rows], weight_ref[...], preferred_element_type=F32)
@@ -67,6 +84,8 @@
     away = [copies.start(panel_ref.at[r], panel_ref.at[r], p) for p in chips]
     beside = [copies.start(panel_ref.at[r], panel_ref.at[r], partner)]
 
+    loads[2].wait()
+    loads[3].wait()
     count = count_ref[0, 0]
     ids = (
         lax.broadcasted_iota(jnp.int32, (8, 16, 128), 0) * 16
@@ -110,61 +129,114 @@
 
 
 def prepare(count, offsets, weights, features, weight):
-    slots = offsets.shape[0]
+    slots = offsets.shape[2]
     vmem = pl.BlockSpec(memory_space=pltpu.VMEM)
+    hbm = pl.BlockSpec(memory_space=pltpu.HBM)
     return pl.pallas_call(
         prepare_kernel,
         out_shape=(
             jax.ShapeDtypeStruct((slots, 128, 128), BF16),
             jax.ShapeDtypeStruct((8, 4, 128, 128), BF16),
         ),
-        in_specs=[pl.BlockSpec(memory_space=pltpu.SMEM)] + [vmem] * 4,
+        in_specs=[pl.BlockSpec(memory_space=pltpu.SMEM)] + [hbm] * 4,
         out_specs=(vmem,) * 2,
-        scratch_shapes=[pltpu.SemaphoreType.DMA((7,)), pltpu.SemaphoreType.DMA((7,))],
+        scratch_shapes=[
+            pltpu.VMEM((slots, 128), jnp.int32),
+            pltpu.VMEM((slots, 128), BF16),
+            pltpu.VMEM((512, 128), BF16),
+            pltpu.VMEM((128, 128), BF16),
+            pltpu.SemaphoreType.DMA((4,)),
+            pltpu.SemaphoreType.DMA((7,)),
+            pltpu.SemaphoreType.DMA((7,)),
+        ],
         compiler_params=pltpu.CompilerParams(
             collective_id=2, has_side_effects=True, vmem_limit_bytes=PREP_VMEM
         ),
         name="prepare",
-    )(count, offsets, weights, features, weight)
-
-
-def forward_kernel(count_ref, row_ref, col_ref, d_ref, x_ref, t_ref):
+    )(count, *in_hbm(offsets, weights, features, weight))
+
+
+def in_hbm(*arrays):
+    return [pltpu.with_memory_space_constraint(a, pltpu.HBM) for a in arrays]
+
+
+def load_tables(row_hbm, col_hbm, row_ref, col_ref, sem):
+    loads = [
+        pltpu.make_async_copy(row_hbm, row_ref, sem.at[0]),
+        pltpu.make_async_copy(col_hbm, col_ref, sem.at[1]),
+    ]
+    for copy in loads:
+        copy.start()
+    return loads
+
+
+def forward_kernel(count_ref, row_hbm, col_hbm, d_ref, x_ref, t_ref, row_ref, col_ref, sem):
+    loads = load_tables(row_hbm, col_hbm, row_ref, col_ref, sem)
     t_ref[...] = jnp.zeros_like(t_ref)
+    for copy in loads:
+        copy.wait()
 
     def step(i, carry):
         for s in range(BATCH):
             n = i * BATCH + s
-            r, c = row_ref[n], col_ref[n]
+            r, c = row_ref[0, 0, n], col_ref[0, 0, n]
             t_ref[r] += jnp.dot(x_ref[c], d_ref[n], preferred_element_type=F32)
         return carry
 
     lax.fori_loop(0, lax.div(count_ref[0, 0] + (BATCH - 1), BATCH), step, 0)
 
 
-def backward_kernel(count_ref, row_ref, col_ref, d_ref, y_ref, t_ref):
+def backward_kernel(
+    count_ref, row_hbm, col_hbm, d_ref, y_ref, result_ref, t_ref, result_hbm, row_ref, col_ref, sem
+):
+    loads = load_tables(row_hbm, col_hbm, row_ref, col_ref, sem)
+    passed = pltpu.make_async_copy(result_ref, result_hbm, sem.at[2])
+    passed.start()
     t_ref[...] = jnp.zeros_like(t_ref)
+    for copy in loads:
+        copy.wait()
 
     def step(i, carry):
         for s in range(BATCH):
             n = i * BATCH + s
-            r, c = row_ref[n], col_ref[n]
+            r, c = row_ref[0, 0, n], col_ref[0, 0, n]
             t_ref[c] += jnp.dot(d_ref[n], y_ref[r], preferred_element_type=F32)
         return carry
 
     lax.fori_loop(0, lax.div(count_ref[0, 0] + (BATCH - 1), BATCH), step, 0)
-
-
-def block_sums(kernel, name, count, brow, bcol, dense, panel, blocks):
-    slots = dense.shape[0]
+    passed.wait()
+
+
+def block_sums(name, count, brow, bcol, dense, panel, blocks, result=None):
     smem, vmem = pl.BlockSpec(memory_space=pltpu.SMEM), pl.BlockSpec(memory_space=pltpu.VMEM)
+    sums = jax.ShapeDtypeStruct((blocks, 128, 128), F32)
+    params = pltpu.CompilerParams(vmem_limit_bytes=SUMS_VMEM)
+    hbm = pl.BlockSpec(memory_space=pltpu.HBM)
+    brow, bcol = in_hbm(brow, bcol)
+    scratch = [
+        pltpu.SMEM(brow.shape, jnp.int32),
+        pltpu.SMEM(bcol.shape, jnp.int32),
+        pltpu.SemaphoreType.DMA((3,)),
+    ]
+    if result is None:
+        return pl.pallas_call(
+            forward_kernel,
+            in_specs=[smem, hbm, hbm] + [vmem] * 2,
+            out_specs=vmem,
+            scratch_shapes=scratch,
+            out_shape=sums,
+            compiler_params=params,
+            name=name,
+        )(count, brow, bcol, dense, panel)
     return pl.pallas_call(
-        kernel,
-        in_specs=[smem] * 3 + [vmem] * 2,
-        out_specs=vmem,
-        out_shape=jax.ShapeDtypeStruct((blocks, 128, 128), F32),
-        compiler_params=pltpu.CompilerParams(vmem_limit_bytes=SUMS_VMEM),
+        backward_kernel,
+        in_specs=[smem, hbm, hbm] + [vmem] * 3,
+        out_specs=(vmem, hbm),
+        out_shape=(sums, jax.ShapeDtypeStruct(result.shape, result.dtype)),
+        scratch_shapes=scratch,
+        compiler_params=params,
         name=name,
-    )(count, brow, bcol, dense, panel)
+    )(count, brow, bcol, dense, panel, result)
 
 
 LEVELS = 32766.0
@@ -363,21 +435,30 @@
 
 def finish_kernel(
     t_ref, feat_ref, weight_ref, bsum_ref, gf_ref, gw_ref, gb_ref,
-    from_core, outgoing, from_chip, local, row_parts, total, col_parts, whole, send, recv,
+    from_core, outgoing, from_chip, local, plane_parts, total, line_parts, whole,
+    lost, plane_lost, total_lost, line_lost, send, recv,
 ):
     here = place()
     x, z, y, h, k = here
-    r, c = lax.axis_index("row"), lax.axis_index("col")
-    row_shifts = [(dh, dk) for dh in range(4) for dk in range(2) if (dh, dk) != (0, 0)]
-    col_shifts = [
-        (dx, dz, dy) for dx in range(4) for dz in range(2) for dy in range(4) if (dx, dz, dy) != (0, 0, 0)
-    ]
-    row_peers = [shifted(here, dh=dh, dk=dk) for dh, dk in row_shifts]
-    col_peers = [shifted(here, dx=dx, dz=dz, dy=dy) for dx, dz, dy in col_shifts]
+    mine, line = x * 4 + y, (h * 2 + k) * 2 + z
+    plane = [
+        (shifted(here, dx=dx, dy=dy), lax.rem(x + dx, 4) * 4 + lax.rem(y + dy, 4))
+        for dx in range(4)
+        for dy in range(4)
+        if (dx, dy) != (0, 0)
+    ]
+    column = [
+        shifted(here, dz=dz, dh=dh, dk=dk)
+        for dh in range(4)
+        for dz in range(2)
+        for dk in range(2)
+        if (dz, dh, dk) != (0, 0, 0)
+    ]
     barrier = pltpu.get_barrier_semaphore()
-    for peer in row_peers + col_peers:
+    for peer in column + [p for p, _ in plane]:
         pl.semaphore_signal(barrier, inc=1, device_id=peer, device_id_type=MESH)
-    pl.semaphore_wait(barrier, len(row_peers) + len(col_peers))
+    lost[...] = jnp.concatenate([bsum_ref[...], jnp.zeros((7, 128), F32)], axis=0)
+    pl.semaphore_wait(barrier, 30)
     copies = Copies(send, recv)
 
     other = 1 - k
@@ -386,11 +467,18 @@
     for dh in (2, 1, 3, 0):
         to = lax.rem(h + dh, 4)
         pairs.append((dh, to, copies.start(t_ref.at[to, other], from_core.at[to], partner)))
+    bias_plane = [copies.start(lost, plane_lost.at[mine], p) for p, _ in plane]
+    plane_lost[mine] = lost[...]
     chips = []
     for dh, to, copy in pairs[:3]:
         copy.wait_recv()
         outgoing[dh - 1] = (t_ref[to, k] + from_core[to]).astype(BF16)
         chips.append(copies.start(outgoing.at[dh - 1], from_chip.at[dh - 1], shifted(here, dh=dh)))
+    for copy in bias_plane:
+        copy.wait_recv()
+    total_lost[...] = sum_of(plane_lost)
+    bias_line = [copies.start(total_lost, line_lost.at[line], p) for p in column]
+    line_lost[line] = total_lost[...]
     pairs[3][2].wait_recv()
     own = t_ref[h, k] + from_core[h]
     for copy in chips:
@@ -398,47 +486,52 @@
     for i in range(3):
         own = own + from_chip[i].astype(F32)
     grad = own.astype(BF16)
-    local[0:128] = lax.dot_general(
+    local[...] = lax.dot_general(
         feat_ref[...], grad, (((0,), (0,)), ((), ())), preferred_element_type=F32
     )
-    local[128:136] = jnp.concatenate([bsum_ref[...], jnp.zeros((7, 128), F32)], axis=0)
-    local[136:192] = jnp.zeros((56, 128), F32)
-
-    def piece(i):
-        return local.at[pl.ds(pl.multiple_of(i * PIECE, 8), PIECE)]
-
-    sent = [copies.start(piece(p[0]), row_parts.at[r], p) for p in row_peers]
+
+    def rows(i):
+        return pl.ds(pl.multiple_of(i * 8, 8), 8)
+
+    sent = [copies.start(local.at[rows(i)], plane_parts.at[mine], p) for p, i in plane]
+    plane_parts[mine] = local[rows(mine)]
     gf_ref[...] = lax.dot_general(
         grad, weight_ref[...], (((1,), (1,)), ((), ())), preferred_element_type=F32
     ).astype(BF16)
-    row_parts[r] = piece(r)[...]
+    scale = 131072.0**-0.5
+    for copy in bias_line:
+        copy.wait_recv()
+    gb_ref[...] = sum_of(line_lost)[0:1] * scale
     for copy in sent:
         copy.wait_recv()
-    acc = row_parts[0]
-    for i in range(1, 8):
-        acc = acc + row_parts[i]
-    total[...] = acc
-    col_parts[c] = acc
-    spread = [copies.start(total, col_parts.at[c], p) for p in col_peers]
+    total[...] = sum_of(plane_parts)
+    spread = [copies.start(total, line_parts.at[line], p) for p in column]
+    line_parts[line] = total[...]
     for copy in spread:
         copy.wait_recv()
-    acc = col_parts[0]
-    for i in range(1, 32):
-        acc = acc + col_parts[i]
-    mine = whole.at[pl.ds(pl.multiple_of(r * PIECE, 8), PIECE)]
-    mine[...] = acc
-    back = [copies.start(mine, mine, p) for p in row_peers]
+    whole[rows(mine)] = sum_of(line_parts) * scale
+    back = [copies.start(whole.at[rows(mine)], whole.at[rows(mine)], p) for p, _ in plane]
     for copy in back:
         copy.wait_recv()
-    scale = 131072.0**-0.5
-    gw_ref[...] = whole[0:128] * scale
-    gb_ref[...] = whole[128:129] * scale
-    for copy in [p[2] for p in pairs] + chips + sent + spread + back:
+    gw_ref[...] = whole[...]
+    for copy in [p[2] for p in pairs] + bias_plane + chips + bias_line + sent + spread + back:
         copy.wait_send()
+
+
+def sum_of(ref):
+    parts = [ref[i] for i in range(ref.shape[0])]
+    while len(parts) > 1:
+        parts = [a + b for a, b in zip(parts[::2], parts[1::2])]
+    return parts[0]
 
 
 def finish(partial, features, weight, bias_sum):
     vmem = pl.BlockSpec(memory_space=pltpu.VMEM)
+    sums = [
+        pltpu.VMEM((16, 8, 128), F32),
+        pltpu.VMEM((8, 128), F32),
+        pltpu.VMEM((16, 8, 128), F32),
+    ]
     return pl.pallas_call(
         finish_kernel,
         out_shape=(
@@ -452,13 +545,13 @@
             pltpu.VMEM((4, 512, 128), F32),
             pltpu.VMEM((3, 512, 128), BF16),
             pltpu.VMEM((3, 512, 128), BF16),
-            pltpu.VMEM((8 * PIECE, 128), F32),
-            pltpu.VMEM((8, PIECE, 128), F32),
-            pltpu.VMEM((PIECE, 128), F32),
-            pltpu.VMEM((32, PIECE, 128), F32),
-            pltpu.VMEM((8 * PIECE, 128), F32),
-            pltpu.SemaphoreType.DMA((56,)),
-            pltpu.SemaphoreType.DMA((56,)),
+            pltpu.VMEM((128, 128), F32),
+            *sums,
+            pltpu.VMEM((128, 128), F32),
+            pltpu.VMEM((8, 128), F32),
+            *sums,
+            pltpu.SemaphoreType.DMA((82,)),
+            pltpu.SemaphoreType.DMA((82,)),
         ],
         compiler_params=pltpu.CompilerParams(
             collective_id=1, has_side_effects=True, vmem_limit_bytes=FINISH_VMEM
@@ -470,16 +563,14 @@
 def shards(
     features, weight, bias, cotangent, block_count, block_rows, block_cols, edge_offsets, edge_weight
 ):
-    brow, bcol = block_rows[0, 0], block_cols[0, 0]
-    dense, panel = prepare(block_count, edge_offsets[0, 0], edge_weight[0, 0], features, weight)
-    totals = block_sums(
-        forward_kernel, "forward", block_count, brow, bcol, dense, panel.reshape(32, 128, 128), 128
-    )
+    tables = (block_count, block_rows, block_cols)
+    dense, panel = prepare(block_count, edge_offsets, edge_weight, features, weight)
+    totals = block_sums("forward", *tables, dense, panel.reshape(32, 128, 128), 128)
     output, grads, bias_sum = reduce_gather(
         totals.reshape(4, 2, 4, 512, 128), bias.reshape(1, 128), cotangent
     )
-    partial = block_sums(
-        backward_kernel, "backward", block_count, brow, bcol, dense, grads.reshape(128, 128, 128), 32
+    partial, output = block_sums(
+        "backward", *tables, dense, grads.reshape(128, 128, 128), 32, output
     )
     grad_features, grad_weight, grad_bias = finish(
         partial.reshape(4, 2, 512, 128), features, weight, bias_sum

time: 166 us -> 151 us (0.910)
  Pallas kernels: 157 us -> 147 us
  local copies, waits for them, and re-layouts: 7.33 us -> 1.82 us
    unnamed x22 -> x11, local copies, waits for them, and re-layouts: 7.33 us -> 1.82 us
    pallas_call x1, Pallas kernels: 52.5 us -> 47.3 us  [finish(): pl.pallas_call(finish_kernel, out_shape=(jax.ShapeDtypeStruct((512, 128),...]
    pallas_call x1, Pallas kernels: 73.3 us -> 71.1 us  [reduce_gather(): pl.pallas_call(reduce_gather_kernel, out_shape=(jax.ShapeDtypeStruct((512...]
where the time goes in v4:
time: 151 us; the launch traced here: 150 us
  Pallas kernels  147 us (97%)
  local copies, waits for them, and re-layouts  1.82 us (1%)
    pallas_call x1, Pallas kernels, reduce_gather(): pl.pallas_call(reduce_gather_kernel, out_shape=(jax.ShapeDtypeStruct((512...  71.1 us
    pallas_call x1, Pallas kernels, finish(): pl.pallas_call(finish_kernel, out_shape=(jax.ShapeDtypeStruct((512, 128),...  47.3 us
    pallas_call x1, Pallas kernels, prepare(): pl.pallas_call(prepare_kernel, out_shape=(jax.ShapeDtypeStruct((slots, 12...  23.4 us

profile of v4, /device:TPU:1, one launch (start us, length us, event | category | flops | bytes accessed | tf_op | source)
XLA Modules:
  0.0 150.4 jit_solution(11365218195670140577)
XLA Ops:
  1.3 23.4 %prepare.1 = (bf16[512,128,128]{2,1,0:T(8,128)(2,1)S(1)}, bf16[8,4,128,128]{3,2,1,0:T(8,128)(2,1)S(1)}) custom-call(s32[1,1]{1,0:T(1,128)S(6)} %copy.16.count_ref, s32[1,1,512,128]{3,2,1,0:T(8,128)} %off_hbm.1, bf16[1,1,512,128]{3,2,1,0:T(8,128)(2,1)} %w_hbm.1, bf16[512,128]{1,0:T(8,128)(2,1)} %feat_ref.1, bf16[128,128]{1,0:T(8,128)(2,1)} %weight_ref.1), custom_call_target="tpu_custom_call" | custom-call | tf_op jit(solution)/shard_map/prepare/pallas_call | solution.py:135
  24.7 0.0 copy-start.1
  24.7 0.0 copy-start.3
  24.8 2.7 %forward.1 = f32[128,128,128]{2,1,0:T(8,128)S(1)} custom-call(s32[1,1]{1,0:T(1,128)S(6)} %copy.16.count_ref, s32[1,1,512]{2,1,0:T(1,128)} %row_hbm.3, s32[1,1,512]{2,1,0:T(1,128)} %col_hbm.3, bf16[512,128,128]{2,1,0:T(8,128)(2,1)S(1)} %get-tuple-element.14.d_ref, bf16[32,128,128]{2,1,0:T(8,128)(2,1)S(1)} %bitcast.9), custom_call_target="tpu_custom_call" | custom-call | tf_op jit(solution)/shard_map/forward/pallas_call | solution.py:222
  27.5 0.0 copy-done.1
  27.5 0.0 copy-done.3
  27.5 71.1 %reduce_gather.1 = (bf16[512,128]{1,0:T(8,128)(2,1)S(1)}, bf16[4,2,4,512,128]{4,3,2,1,0:T(8,128)(2,1)S(1)}, f32[1,128]{1,0:T(1,128)S(1)}) custom-call(f32[4,2,4,512,128]{4,3,2,1,0:T(8,128)S(1)} %bitcast.6, f32[1,128]{1,0:T(1,128)S(1)} %bitcast.10, bf16[512,128]{1,0:T(8,128)(2,1)S(1)} %copy-done.1), custom_call_target="tpu_custom_call" | custom-call | tf_op jit(solution)/shard_map/reduce_gather/pallas_call | solution.py:413
  98.7 0.0 copy-start
  98.7 0.0 copy-start.2
  98.7 2.7 %backward.1 = (f32[32,128,128]{2,1,0:T(8,128)S(1)}, bf16[512,128]{1,0:T(8,128)(2,1)}) custom-call(s32[1,1]{1,0:T(1,128)S(6)} %copy.16.count_ref, s32[1,1,512]{2,1,0:T(1,128)} %row_hbm.3, s32[1,1,512]{2,1,0:T(1,128)} %col_hbm.3, bf16[512,128,128]{2,1,0:T(8,128)(2,1)S(1)} %get-tuple-element.14.d_ref, bf16[128,128,128]{2,1,0:T(8,128)(2,1)S(1)} %bitcast.7, ...), custom_call_target="tpu_custom_call" | custom-call | tf_op jit(solution)/shard_map/backward/pallas_call | solution.py:231
  101.3 0.0 copy-done
  101.4 0.0 copy-done.2
  101.4 47.3 %finish.1 = (bf16[512,128]{1,0:T(8,128)(2,1)S(1)}, f32[128,128]{1,0:T(8,128)S(1)}, f32[1,128]{1,0:T(1,128)S(1)}) custom-call(f32[4,2,512,128]{3,2,1,0:T(8,128)S(1)} %bitcast.8, bf16[512,128]{1,0:T(8,128)(2,1)S(1)} %copy-done, bf16[128,128]{1,0:T(8,128)(2,1)S(1)} %copy-done.2, f32[1,128]{1,0:T(1,128)S(1)} %get-tuple-element.20.bsum_ref), custom_call_target="tpu_custom_call" | custom-call | tf_op jit(solution)/shard_map/finish/pallas_call | solution.py:535
  148.6 0.7 copy.17
  149.3 0.6 copy.18
  149.9 0.5 copy.19
Async XLA Ops:
  24.7 2.8 %copy-start.1 = (bf16[512,128]{1,0:T(8,128)(2,1)S(1)}, bf16[512,128]{1,0:T(8,128)(2,1)}, u32[]{:S(2)}) copy-start(bf16[512,128]{1,0:T(8,128)(2,1)} %cot_ref.1) | copy-start | bytes 393220
  24.7 2.8 %copy-start.3 = (f32[128]{0:T(128)S(1)}, f32[128]{0:T(128)}, u32[]{:S(2)}) copy-start(f32[128]{0:T(128)} %param.11) | copy-start | bytes 1540
  98.7 2.7 %copy-start = (bf16[512,128]{1,0:T(8,128)(2,1)S(1)}, bf16[512,128]{1,0:T(8,128)(2,1)}, u32[]{:S(2)}) copy-start(bf16[512,128]{1,0:T(8,128)(2,1)} %feat_ref.1) | copy-start | bytes 393220
  98.7 2.7 %copy-start.2 = (bf16[128,128]{1,0:T(8,128)(2,1)S(1)}, bf16[128,128]{1,0:T(8,128)(2,1)}, u32[]{:S(2)}) copy-start(bf16[128,128]{1,0:T(8,128)(2,1)} %weight_ref.1) | copy-start | bytes 98308

commit v5 on v4

--- a/solution.py
+++ b/solution.py
@@ -28,6 +28,27 @@
     x, z, y = lax.rem(x + dx, 4), lax.rem(z + dz, 2), lax.rem(y + dy, 4)
     h, k = lax.rem(h + dh, 4), lax.rem(k + dk, 2)
     return (h * 2 + k, x * 8 + z * 4 + y)
+
+
+class RingGather:
+    def __init__(self, copies, mine, from_minus, from_plus, plus, minus):
+        self.copies, self.plus, self.minus = copies, plus, minus
+        self.from_minus, self.from_plus = from_minus, from_plus
+        self.sent = [copies.start(mine, mine, plus), copies.start(mine, mine, minus)]
+
+    def pass_on(self):
+        self.sent[0].wait_recv()
+        self.sent.append(self.copies.start(self.from_minus, self.from_minus, self.plus))
+        self.sent[1].wait_recv()
+        self.sent.append(self.copies.start(self.from_plus, self.from_plus, self.minus))
+
+    def arrive(self):
+        self.sent[2].wait_recv()
+        self.sent[3].wait_recv()
+
+    def drain(self):
+        for copy in self.sent:
+            copy.wait_send()
 
 
 class Copies:
@@ -69,9 +90,9 @@
     x, z, y, h, k = here
     r = lax.axis_index("row")
     partner = shifted(here, dk=1)
-    chips = [shifted(here, dh=dh) for dh in (2, 1, 3)]
+    above, below = shifted(here, dh=1), shifted(here, dh=3)
     barrier = pltpu.get_barrier_semaphore()
-    for peer in [partner] + chips:
+    for peer in (partner, above, below):
         pl.semaphore_signal(barrier, inc=1, device_id=peer, device_id_type=MESH)
     loads[0].wait()
     loads[1].wait()
@@ -79,10 +100,17 @@
         rows = slice(b * 128, (b + 1) * 128)
         projected = jnp.dot(feat_ref[rows], weight_ref[...], preferred_element_type=F32)
         panel_ref[r, b] = projected.T.astype(BF16)
-    pl.semaphore_wait(barrier, 4)
+    pl.semaphore_wait(barrier, 3)
     copies = Copies(send, recv)
-    away = [copies.start(panel_ref.at[r], panel_ref.at[r], p) for p in chips]
-    beside = [copies.start(panel_ref.at[r], panel_ref.at[r], partner)]
+    h1, h2, h3 = (lax.rem(h + i, 4) * 2 + k for i in (1, 2, 3))
+    ring = RingGather(
+        copies, panel_ref.at[r], panel_ref.at[h3, 0:2], panel_ref.at[h1, 2:4], above, below
+    )
+
+    def pass_over(i):
+        return copies.start(panel_ref.at[i], panel_ref.at[i], partner)
+
+    beside = [pass_over(r)]
 
     loads[2].wait()
     loads[3].wait()
@@ -116,16 +144,16 @@
         return carry
 
     steps = d_ref.shape[0] // BATCH
-    lax.fori_loop(0, steps * 3 // 4, densify, 0)
-    for dh, copy in zip((2, 1, 3), away):
-        copy.wait_recv()
-        got = panel_ref.at[lax.rem(h - dh + 4, 4) * 2 + k]
-        beside.append(copies.start(got, got, partner))
-    lax.fori_loop(steps * 3 // 4, steps, densify, 0)
+    lax.fori_loop(0, steps // 2, densify, 0)
+    ring.pass_on()
+    beside += [pass_over(h3), pass_over(h1)]
+    lax.fori_loop(steps // 2, steps * 7 // 8, densify, 0)
+    ring.arrive()
+    beside.append(pass_over(h2))
+    lax.fori_loop(steps * 7 // 8, steps, densify, 0)
     for copy in beside:
-        copy.wait_recv()
-    for copy in away + beside:
-        copy.wait_send()
+        copy.wait()
+    ring.drain()
 
 
 def prepare(count, offsets, weights, features, weight):
@@ -146,8 +174,8 @@
             pltpu.VMEM((512, 128), BF16),
             pltpu.VMEM((128, 128), BF16),
             pltpu.SemaphoreType.DMA((4,)),
-            pltpu.SemaphoreType.DMA((7,)),
-            pltpu.SemaphoreType.DMA((7,)),
+            pltpu.SemaphoreType.DMA((8,)),
+            pltpu.SemaphoreType.DMA((8,)),
         ],
         compiler_params=pltpu.CompilerParams(
             collective_id=2, has_side_effects=True, vmem_limit_bytes=PREP_VMEM
@@ -356,48 +384,67 @@
             g_ref[x, z, y, rows] = grad.astype(BF16)
     bsum_ref[...] = lost
 
-    copies.start(g_ref.at[x, z, y], g_ref.at[x, z, y], zp).wait()
-    top, low = pl.ds(0, 256), pl.ds(256, 256)
-    x1, x3 = lax.rem(x + 1, 4), lax.rem(x + 3, 4)
-    y1, y3 = lax.rem(y + 1, 4), lax.rem(y + 3, 4)
-
-    def ring_gather(mine, before, after, plus, minus):
-        sent = [copies.start(mine, mine, plus), copies.start(mine, mine, minus)]
-
-        def middle():
-            sent[0].wait_recv()
-            sent.append(copies.start(before, before, plus))
-            sent[1].wait_recv()
-            sent.append(copies.start(after, after, minus))
-
-        def last():
-            sent[2].wait_recv()
-            sent[3].wait_recv()
-            for copy in sent:
-                copy.wait_send()
-
-        return middle, last
-
-    mid_a, end_a = ring_gather(
-        g_ref.at[x, :, y, top], g_ref.at[x, 0, y3, top], g_ref.at[x, 1, y1, top], yp, ym
-    )
-    mid_b, end_b = ring_gather(
-        g_ref.at[x, :, y, low], g_ref.at[x3, 0, y, low], g_ref.at[x1, 1, y, low], xp, xm
-    )
-    mid_a()
-    mid_b()
-    end_a()
-    mid_c, end_c = ring_gather(
-        g_ref.at[x, :, :, top], g_ref.at[x3, 0, :, top], g_ref.at[x1, 1, :, top], xp, xm
-    )
-    end_b()
-    mid_d, end_d = ring_gather(
-        g_ref.at[:, :, y, low], g_ref.at[:, 0, y3, low], g_ref.at[:, 1, y1, low], yp, ym
-    )
-    mid_c()
-    mid_d()
-    end_c()
-    end_d()
+    half_a, half_b, late_a, late_b = pl.ds(0, 192), pl.ds(192, 192), pl.ds(384, 64), pl.ds(448, 64)
+    x1, x2, x3 = (lax.rem(x + i, 4) for i in (1, 2, 3))
+    y1, y2, y3 = (lax.rem(y + i, 4) for i in (1, 2, 3))
+
+    def over_z(ref):
+        return copies.start(ref, ref, zp)
+
+    first_z = over_z(g_ref.at[x, z, y, 0:384])
+    near_e = RingGather(
+        copies, g_ref.at[x, z, y, late_a], g_ref.at[x, z, y3, 384:416], g_ref.at[x, z, y1, 416:448], yp, ym
+    )
+    near_f = RingGather(
+        copies, g_ref.at[x, z, y, late_b], g_ref.at[x3, z, y, 448:480], g_ref.at[x1, z, y, 480:512], xp, xm
+    )
+    first_z.wait_recv()
+    near_a = RingGather(
+        copies, g_ref.at[x, :, y, half_a], g_ref.at[x, 0, y3, half_a], g_ref.at[x, 1, y1, half_a], yp, ym
+    )
+    near_b = RingGather(
+        copies, g_ref.at[x, :, y, half_b], g_ref.at[x3, 0, y, half_b], g_ref.at[x1, 1, y, half_b], xp, xm
+    )
+    near_e.pass_on()
+    near_f.pass_on()
+    near_a.pass_on()
+    near_b.pass_on()
+    near_e.arrive()
+    far_e = RingGather(
+        copies, g_ref.at[x, z, :, late_a], g_ref.at[x3, z, 0:2, late_a], g_ref.at[x1, z, 2:4, late_a], xp, xm
+    )
+    last_z = [over_z(g_ref.at[x, z, :, late_a])]
+    near_f.arrive()
+    far_f = RingGather(
+        copies, g_ref.at[:, z, y, late_b], g_ref.at[0:2, z, y3, late_b], g_ref.at[2:4, z, y1, late_b], yp, ym
+    )
+    last_z.append(over_z(g_ref.at[:, z, y, late_b]))
+    near_a.arrive()
+    far_a = RingGather(
+        copies, g_ref.at[x, :, :, half_a], g_ref.at[x3, 0, :, half_a], g_ref.at[x1, 1, :, half_a], xp, xm
+    )
+    near_b.arrive()
+    far_b = RingGather(
+        copies, g_ref.at[:, :, y, half_b], g_ref.at[:, 0, y3, half_b], g_ref.at[:, 1, y1, half_b], yp, ym
+    )
+    far_e.pass_on()
+    last_z += [over_z(g_ref.at[x3, z, :, late_a]), over_z(g_ref.at[x1, z, :, late_a])]
+    far_f.pass_on()
+    last_z += [over_z(g_ref.at[:, z, y3, late_b]), over_z(g_ref.at[:, z, y1, late_b])]
+    far_e.arrive()
+    last_z.append(over_z(g_ref.at[x2, z, :, late_a]))
+    far_f.arrive()
+    last_z.append(over_z(g_ref.at[:, z, y2, late_b]))
+    far_a.pass_on()
+    far_b.pass_on()
+    far_a.arrive()
+    far_b.arrive()
+    for copy in last_z:
+        copy.wait_recv()
+    for copy in [first_z] + last_z:
+        copy.wait_send()
+    for ring in (near_a, near_b, near_e, near_f, far_a, far_b, far_e, far_f):
+        ring.drain()
 
 
 def reduce_gather(totals, bias, cotangent):
@@ -423,8 +470,8 @@
         + ring((256, 128)) * 2
         + [
             pltpu.VMEM((2, 256, 128), F32),
-            pltpu.SemaphoreType.DMA((72,)),
-            pltpu.SemaphoreType.DMA((72,)),
+            pltpu.SemaphoreType.DMA((92,)),
+            pltpu.SemaphoreType.DMA((92,)),
         ],
         compiler_params=pltpu.CompilerParams(
             collective_id=0, has_side_effects=True, vmem_limit_bytes=REDUCE_VMEM
@@ -463,28 +510,50 @@
 
     other = 1 - k
     partner = shifted(here, dk=1)
-    pairs = []
+    pairs = {}
     for dh in (2, 1, 3, 0):
         to = lax.rem(h + dh, 4)
-        pairs.append((dh, to, copies.start(t_ref.at[to, other], from_core.at[to], partner)))
+        pairs[dh] = copies.start(t_ref.at[to, other], from_core.at[to], partner)
     bias_plane = [copies.start(lost, plane_lost.at[mine], p) for p, _ in plane]
     plane_lost[mine] = lost[...]
+    above, below = shifted(here, dh=1), shifted(here, dh=3)
     chips = []
-    for dh, to, copy in pairs[:3]:
-        copy.wait_recv()
-        outgoing[dh - 1] = (t_ref[to, k] + from_core[to]).astype(BF16)
-        chips.append(copies.start(outgoing.at[dh - 1], from_chip.at[dh - 1], shifted(here, dh=dh)))
+
+    def both(dh, part):
+        to = lax.rem(h + dh, 4)
+        return t_ref[to, k, part] + from_core[to, part]
+
+    def send(value, slot, device):
+        outgoing[slot] = value.astype(BF16)
+        chips.append(copies.start(outgoing.at[slot], from_chip.at[slot], device))
+
+    upper, lower = slice(0, 256), slice(256, 512)
+    pairs[2].wait_recv()
+    send(both(2, upper), 0, above)
+    send(both(2, lower), 1, below)
+    pairs[1].wait_recv()
+    send(both(1, lower), 2, above)
+    pairs[3].wait_recv()
+    send(both(3, upper), 3, below)
     for copy in bias_plane:
         copy.wait_recv()
     total_lost[...] = sum_of(plane_lost)
     bias_line = [copies.start(total_lost, line_lost.at[line], p) for p in column]
     line_lost[line] = total_lost[...]
-    pairs[3][2].wait_recv()
-    own = t_ref[h, k] + from_core[h]
-    for copy in chips:
+    pairs[0].wait_recv()
+    chips[0].wait_recv()
+    send(both(1, upper) + from_chip[0].astype(F32), 4, above)
+    chips[1].wait_recv()
+    send(both(3, lower) + from_chip[1].astype(F32), 5, below)
+    for copy in chips[2:]:
         copy.wait_recv()
-    for i in range(3):
-        own = own + from_chip[i].astype(F32)
+    own = jnp.concatenate(
+        [
+            both(0, upper) + from_chip[3].astype(F32) + from_chip[4].astype(F32),
+            both(0, lower) + from_chip[2].astype(F32) + from_chip[5].astype(F32),
+        ],
+        axis=0,
+    )
     grad = own.astype(BF16)
     local[...] = lax.dot_general(
         feat_ref[...], grad, (((0,), (0,)), ((), ())), preferred_element_type=F32
@@ -514,7 +583,7 @@
     for copy in back:
         copy.wait_recv()
     gw_ref[...] = whole[...]
-    for copy in [p[2] for p in pairs] + bias_plane + chips + bias_line + sent + spread + back:
+    for copy in [pairs[dh] for dh in range(4)] + bias_plane + chips + bias_line + sent + spread + back:
         copy.wait_send()
 
 
@@ -543,15 +612,15 @@
         out_specs=(vmem,) * 3,
         scratch_shapes=[
             pltpu.VMEM((4, 512, 128), F32),
-            pltpu.VMEM((3, 512, 128), BF16),
-            pltpu.VMEM((3, 512, 128), BF16),
+            pltpu.VMEM((6, 256, 128), BF16),
+            pltpu.VMEM((6, 256, 128), BF16),
             pltpu.VMEM((128, 128), F32),
             *sums,
             pltpu.VMEM((128, 128), F32),
             pltpu.VMEM((8, 128), F32),
             *sums,
-            pltpu.SemaphoreType.DMA((82,)),
-            pltpu.SemaphoreType.DMA((82,)),
+            pltpu.SemaphoreType.DMA((85,)),
+            pltpu.SemaphoreType.DMA((85,)),
         ],
         compiler_params=pltpu.CompilerParams(
             collective_id=1, has_side_effects=True, vmem_limit_bytes=FINISH_VMEM

time: 151 us -> 142 us (0.940)
  Pallas kernels: 147 us -> 139 us
    pallas_call x1, Pallas kernels: 47.3 us -> 44.2 us  [finish(): pl.pallas_call(finish_kernel, out_shape=(jax.ShapeDtypeStruct((512, 128),...]
    pallas_call x1, Pallas kernels: 71.1 us -> 68.3 us  [reduce_gather(): pl.pallas_call(reduce_gather_kernel, out_shape=(jax.ShapeDtypeStruct((512...]
    pallas_call x1, Pallas kernels: 23.4 us -> 21.3 us  [prepare(): pl.pallas_call(prepare_kernel, out_shape=(jax.ShapeDtypeStruct((slots, 12...]
where the time goes in v5:
time: 142 us
  Pallas kernels  139 us (98%)
  local copies, waits for them, and re-layouts  1.82 us (1%)
    pallas_call x1, Pallas kernels, reduce_gather(): pl.pallas_call(reduce_gather_kernel, out_shape=(jax.ShapeDtypeStruct((512...  68.3 us
    pallas_call x1, Pallas kernels, finish(): pl.pallas_call(finish_kernel, out_shape=(jax.ShapeDtypeStruct((512, 128),...  44.2 us
    pallas_call x1, Pallas kernels, prepare(): pl.pallas_call(prepare_kernel, out_shape=(jax.ShapeDtypeStruct((slots, 12...  21.3 us

profile of v5, /device:TPU:1, one launch (start us, length us, event | category | flops | bytes accessed | tf_op | source)
XLA Modules:
  0.0 142.3 jit_solution(5825139386580230979)
XLA Ops:
  1.3 21.3 %prepare.1 = (bf16[512,128,128]{2,1,0:T(8,128)(2,1)S(1)}, bf16[8,4,128,128]{3,2,1,0:T(8,128)(2,1)S(1)}) custom-call(s32[1,1]{1,0:T(1,128)S(6)} %copy.16.count_ref, s32[1,1,512,128]{3,2,1,0:T(8,128)} %off_hbm.1, bf16[1,1,512,128]{3,2,1,0:T(8,128)(2,1)} %w_hbm.1, bf16[512,128]{1,0:T(8,128)(2,1)} %feat_ref.1, bf16[128,128]{1,0:T(8,128)(2,1)} %weight_ref.1), custom_call_target="tpu_custom_call" | custom-call | tf_op jit(solution)/shard_map/prepare/pallas_call | solution.py:163
  22.5 0.0 copy-start.1
  22.6 0.0 copy-start.3
  22.6 2.7 %forward.1 = f32[128,128,128]{2,1,0:T(8,128)S(1)} custom-call(s32[1,1]{1,0:T(1,128)S(6)} %copy.16.count_ref, s32[1,1,512]{2,1,0:T(1,128)} %row_hbm.3, s32[1,1,512]{2,1,0:T(1,128)} %col_hbm.3, bf16[512,128,128]{2,1,0:T(8,128)(2,1)S(1)} %get-tuple-element.14.d_ref, bf16[32,128,128]{2,1,0:T(8,128)(2,1)S(1)} %bitcast.9), custom_call_target="tpu_custom_call" | custom-call | tf_op jit(solution)/shard_map/forward/pallas_call | solution.py:250
  25.3 0.0 copy-done.1
  25.3 0.0 copy-done.3
  25.3 68.3 %reduce_gather.1 = (bf16[512,128]{1,0:T(8,128)(2,1)S(1)}, bf16[4,2,4,512,128]{4,3,2,1,0:T(8,128)(2,1)S(1)}, f32[1,128]{1,0:T(1,128)S(1)}) custom-call(f32[4,2,4,512,128]{4,3,2,1,0:T(8,128)S(1)} %bitcast.6, f32[1,128]{1,0:T(1,128)S(1)} %bitcast.10, bf16[512,128]{1,0:T(8,128)(2,1)S(1)} %copy-done.1), custom_call_target="tpu_custom_call" | custom-call | tf_op jit(solution)/shard_map/reduce_gather/pallas_call | solution.py:460
  93.6 0.0 copy-start
  93.6 0.0 copy-start.2
  93.6 2.7 %backward.1 = (f32[32,128,128]{2,1,0:T(8,128)S(1)}, bf16[512,128]{1,0:T(8,128)(2,1)}) custom-call(s32[1,1]{1,0:T(1,128)S(6)} %copy.16.count_ref, s32[1,1,512]{2,1,0:T(1,128)} %row_hbm.3, s32[1,1,512]{2,1,0:T(1,128)} %col_hbm.3, bf16[512,128,128]{2,1,0:T(8,128)(2,1)S(1)} %get-tuple-element.14.d_ref, bf16[128,128,128]{2,1,0:T(8,128)(2,1)S(1)} %bitcast.7, ...), custom_call_target="tpu_custom_call" | custom-call | tf_op jit(solution)/shard_map/backward/pallas_call | solution.py:259
  96.3 0.0 copy-done
  96.3 0.0 copy-done.2
  96.3 44.2 %finish.1 = (bf16[512,128]{1,0:T(8,128)(2,1)S(1)}, f32[128,128]{1,0:T(8,128)S(1)}, f32[1,128]{1,0:T(1,128)S(1)}) custom-call(f32[4,2,512,128]{3,2,1,0:T(8,128)S(1)} %bitcast.8, bf16[512,128]{1,0:T(8,128)(2,1)S(1)} %copy-done, bf16[128,128]{1,0:T(8,128)(2,1)S(1)} %copy-done.2, f32[1,128]{1,0:T(1,128)S(1)} %get-tuple-element.20.bsum_ref), custom_call_target="tpu_custom_call" | custom-call | tf_op jit(solution)/shard_map/finish/pallas_call | solution.py:604
  140.5 0.7 copy.17
  141.2 0.6 copy.18
  141.8 0.5 copy.19
Async XLA Ops:
  22.5 2.8 %copy-start.1 = (bf16[512,128]{1,0:T(8,128)(2,1)S(1)}, bf16[512,128]{1,0:T(8,128)(2,1)}, u32[]{:S(2)}) copy-start(bf16[512,128]{1,0:T(8,128)(2,1)} %cot_ref.1) | copy-start | bytes 393220
  22.6 2.8 %copy-start.3 = (f32[128]{0:T(128)S(1)}, f32[128]{0:T(128)}, u32[]{:S(2)}) copy-start(f32[128]{0:T(128)} %param.11) | copy-start | bytes 1540
  93.6 2.7 %copy-start = (bf16[512,128]{1,0:T(8,128)(2,1)S(1)}, bf16[512,128]{1,0:T(8,128)(2,1)}, u32[]{:S(2)}) copy-start(bf16[512,128]{1,0:T(8,128)(2,1)} %feat_ref.1) | copy-start | bytes 393220
  93.6 2.7 %copy-start.2 = (bf16[128,128]{1,0:T(8,128)(2,1)S(1)}, bf16[128,128]{1,0:T(8,128)(2,1)}, u32[]{:S(2)}) copy-start(bf16[128,128]{1,0:T(8,128)(2,1)} %weight_ref.1) | copy-start | bytes 98308

commit v6 on v5

--- a/solution.py
+++ b/solution.py
@@ -272,8 +272,8 @@
 
 def blocks_of(ref):
     if len(ref.shape) == 2:
-        return [(pl.ds(128 * b, 128),) for b in range(2)]
-    return [(i, pl.ds(128 * b, 128)) for i in range(ref.shape[0]) for b in range(2)]
+        return [(Ellipsis,)]
+    return [(i, Ellipsis) for i in range(ref.shape[0])]
 
 
 def encode(value, at, n, q_ref, s_ref):
@@ -286,61 +286,69 @@
 
 def decode(at, n, q_ref, s_ref):
     level = q_ref[at].astype(jnp.int32).astype(F32)
-    return level * jnp.abs(level) * s_ref[n : n + 1]
-
-
-def ring_sum(copies, pick, me, plus, minus, q, scales, total):
-    p1, p2, p3 = lax.rem(me + 1, 4), lax.rem(me + 2, 4), lax.rem(me + 3, 4)
-
-    def send(value, slot, device):
-        for n, at in enumerate(blocks_of(q.at[slot])):
-            encode(value(n, at), at, n, q.at[slot], scales.at[slot])
+    return level * jnp.abs(level) * s_ref[pl.ds(n, 1)]
+
+
+class RingSum:
+    def __init__(self, copies, value, me, plus, minus, q, scales):
+        self.copies, self.value, self.q, self.scales = copies, value, q, scales
+        self.me, self.p1, self.p2, self.p3 = me, lax.rem(me + 1, 4), lax.rem(me + 2, 4), lax.rem(me + 3, 4)
+        self.plus, self.minus = plus, minus
+        self.sent = {}
+
+    def code(self, value, slot):
+        for n, at in enumerate(blocks_of(self.q.at[slot])):
+            encode(value(n, at), at, n, self.q.at[slot], self.scales.at[slot])
+
+    def start(self, slot, device):
+        self.sent[slot] = (
+            self.copies.start(self.q.at[slot], self.q.at[slot + 6], device),
+            self.copies.start(self.scales.at[slot], self.scales.at[slot + 6], device),
+        )
+
+    def got(self, slot, n, at):
+        return decode(at, n, self.q.at[slot + 6], self.scales.at[slot + 6])
+
+    def wait(self, *slots):
+        for slot in slots:
+            for copy in self.sent[slot]:
+                copy.wait_recv()
+
+    def code_far(self, half):
+        self.code(self.value(self.p2, half), half)
+
+    def send_far(self, half):
+        self.start(half, (self.plus, self.minus)[half])
+
+    def send_near(self, half):
+        self.code(self.value((self.p3, self.p1)[half], half), 3 - half)
+        self.start(3 - half, (self.minus, self.plus)[half])
+
+    def pass_on(self, half):
+        self.wait(half)
+        own = self.value((self.p1, self.p3)[half], half)
+        self.code(lambda n, at: own(n, at) + self.got(half, n, at), half + 4)
+        self.start(half + 4, (self.plus, self.minus)[half])
+
+    def arrive(self):
+        self.wait(2, 3, 4, 5)
+
+    def total(self, half, n, at):
         return (
-            copies.start(q.at[slot], q.at[slot + 6], device),
-            copies.start(scales.at[slot], scales.at[slot + 6], device),
-        )
-
-    def got(slot):
-        return lambda n, at: decode(at, n, q.at[slot + 6], scales.at[slot + 6])
-
-    def own(p, half):
-        return lambda n, at: pick(p, half)[at]
-
-    def plus_got(p, half, slot):
-        return lambda n, at: own(p, half)(n, at) + got(slot)(n, at)
-
-    first = [
-        send(own(p2, 0), 0, plus),
-        send(own(p2, 1), 1, minus),
-        send(own(p1, 1), 2, plus),
-        send(own(p3, 0), 3, minus),
-    ]
-
-    def middle():
-        second = []
-        for slot, p, half, device in ((0, p1, 0, plus), (1, p3, 1, minus)):
-            for copy in first[slot]:
-                copy.wait_recv()
-            second.append(send(plus_got(p, half, slot), slot + 4, device))
-        return second
-
-    def last(second):
-        for half, one, two in ((1, 2, 5), (0, 3, 4)):
-            for copy in first[one] + second[two - 4]:
-                copy.wait_recv()
-            out = total.at[half]
-            for n, at in enumerate(blocks_of(out)):
-                out[at] = own(me, half)(n, at) + got(one)(n, at) + got(two)(n, at)
-        for pair in first + second:
+            self.value(self.me, half)(n, at)
+            + self.got(3 - half, n, at)
+            + self.got(half + 4, n, at)
+        )
+
+    def drain(self):
+        for pair in self.sent.values():
             for copy in pair:
                 copy.wait_send()
 
-    return middle, last
-
 
 def reduce_gather_kernel(
     t_ref, bias_ref, cot_ref, out_ref, g_ref, bsum_ref,
-    q_a, scale_a, sum_a, q_b, scale_b, sum_b, q_c, scale_c, sum_c, q_d, scale_d, sum_d, pair, send, recv,
+    first_q, first_scale, second_q, second_scale, sums, pair, send, recv,
 ):
     here = place()
     x, z, y, h, k = here
@@ -350,113 +358,152 @@
     barrier = pltpu.get_barrier_semaphore()
     for peer in (xp, xm, yp, ym, zp):
         pl.semaphore_signal(barrier, inc=1, device_id=peer, device_id_type=MESH)
-    pl.semaphore_wait(barrier, 5)
     copies = Copies(send, recv)
 
-    mid_a, end_a = ring_sum(
-        copies, lambda p, q: t_ref.at[p, q, :, 0:256, :], x, xp, xm, q_a, scale_a, sum_a
-    )
-    mid_b, end_b = ring_sum(
-        copies, lambda p, q: t_ref.at[:, q, p, 256:512, :], y, yp, ym, q_b, scale_b, sum_b
-    )
-    second_a, second_b = mid_a(), mid_b()
-    end_a(second_a)
-    mid_c, end_c = ring_sum(copies, lambda p, q: sum_a.at[q, p], y, yp, ym, q_c, scale_c, sum_c)
-    end_b(second_b)
-    mid_d, end_d = ring_sum(copies, lambda p, q: sum_b.at[q, p], x, xp, xm, q_d, scale_d, sum_d)
-    second_c, second_d = mid_c(), mid_d()
+    def ring_over_x(number, q, scale, value):
+        return RingSum(copies, value, x, xp, xm, q.at[number], scale.at[number])
+
+    def ring_over_y(number, q, scale, value):
+        return RingSum(copies, value, y, yp, ym, q.at[number], scale.at[number])
+
+    def part_a(b):
+        rows = slice(b * 128, (b + 1) * 128)
+        return lambda p, half: lambda n, at: t_ref.at[p, half, :, rows, :][at]
+
+    def part_b(b):
+        rows = slice((2 + b) * 128, (3 + b) * 128)
+        return lambda p, half: lambda n, at: t_ref.at[:, half, p, rows, :][at]
+
+    def then(ring):
+        return lambda p, half: lambda n, at: ring.total(half, p, (p, Ellipsis))
+
+    first, second = [], []
+    for b in range(2):
+        over_x = ring_over_x(2 * b, first_q, first_scale, part_a(b))
+        over_y = ring_over_y(2 * b + 1, first_q, first_scale, part_b(b))
+        first.append((over_x, over_y))
+        second.append(
+            (
+                ring_over_y(2 * b, second_q, second_scale, then(over_x)),
+                ring_over_x(2 * b + 1, second_q, second_scale, then(over_y)),
+            )
+        )
+
+    def each(rings, *steps):
+        for half in range(2):
+            for ring in rings:
+                for step in steps:
+                    getattr(ring, step)(half)
+
+    def arrive(rings):
+        for ring in rings:
+            ring.arrive()
+
+    def start(rings):
+        each(rings, "code_far", "send_far")
+        each(rings, "send_near")
+
     other = 1 - z
-    end_c(second_c)
-    pair_c = copies.start(sum_c.at[other], pair.at[0], zp)
-    end_d(second_d)
-    pair_d = copies.start(sum_d.at[other], pair.at[1], zp)
+
+    def pair_up(b):
+        for i, ring in enumerate(second[b]):
+            for half in range(2):
+                sums[b, half, i] = ring.total(half, 0, (Ellipsis,))
+        return copies.start(sums.at[b, other], pair.at[b], zp)
+
     bias = bias_ref[...]
-    lost = jnp.zeros((1, 128), F32)
-    for i, (copy, total) in enumerate(((pair_c, sum_c), (pair_d, sum_d))):
-        copy.wait()
-        own = total[z] + pair[i]
-        for b in range(2):
-            pre = own[b * 128 : (b + 1) * 128].T + bias
+
+    def owner(b, lost):
+        for i in range(2):
+            pre = (sums[b, z, i] + pair[b, i]).T + bias
             rows = slice((2 * i + b) * 128, (2 * i + b + 1) * 128)
             out_ref[rows] = jnp.maximum(pre, 0.0).astype(BF16)
             grad = jnp.where(pre > 0, cot_ref[rows].astype(F32), 0.0)
             lost = lost + jnp.sum(grad, axis=0, keepdims=True)
             g_ref[x, z, y, rows] = grad.astype(BF16)
-    bsum_ref[...] = lost
-
-    half_a, half_b, late_a, late_b = pl.ds(0, 192), pl.ds(192, 192), pl.ds(384, 64), pl.ds(448, 64)
-    x1, x2, x3 = (lax.rem(x + i, 4) for i in (1, 2, 3))
-    y1, y2, y3 = (lax.rem(y + i, 4) for i in (1, 2, 3))
-
-    def over_z(ref):
-        return copies.start(ref, ref, zp)
-
-    first_z = over_z(g_ref.at[x, z, y, 0:384])
-    near_e = RingGather(
-        copies, g_ref.at[x, z, y, late_a], g_ref.at[x, z, y3, 384:416], g_ref.at[x, z, y1, 416:448], yp, ym
-    )
-    near_f = RingGather(
-        copies, g_ref.at[x, z, y, late_b], g_ref.at[x3, z, y, 448:480], g_ref.at[x1, z, y, 480:512], xp, xm
-    )
-    first_z.wait_recv()
-    near_a = RingGather(
-        copies, g_ref.at[x, :, y, half_a], g_ref.at[x, 0, y3, half_a], g_ref.at[x, 1, y1, half_a], yp, ym
-    )
-    near_b = RingGather(
-        copies, g_ref.at[x, :, y, half_b], g_ref.at[x3, 0, y, half_b], g_ref.at[x1, 1, y, half_b], xp, xm
-    )
-    near_e.pass_on()
-    near_f.pass_on()
-    near_a.pass_on()
-    near_b.pass_on()
-    near_e.arrive()
-    far_e = RingGather(
-        copies, g_ref.at[x, z, :, late_a], g_ref.at[x3, z, 0:2, late_a], g_ref.at[x1, z, 2:4, late_a], xp, xm
-    )
-    last_z = [over_z(g_ref.at[x, z, :, late_a])]
-    near_f.arrive()
-    far_f = RingGather(
-        copies, g_ref.at[:, z, y, late_b], g_ref.at[0:2, z, y3, late_b], g_ref.at[2:4, z, y1, late_b], yp, ym
-    )
-    last_z.append(over_z(g_ref.at[:, z, y, late_b]))
-    near_a.arrive()
-    far_a = RingGather(
-        copies, g_ref.at[x, :, :, half_a], g_ref.at[x3, 0, :, half_a], g_ref.at[x1, 1, :, half_a], xp, xm
-    )
-    near_b.arrive()
-    far_b = RingGather(
-        copies, g_ref.at[:, :, y, half_b], g_ref.at[:, 0, y3, half_b], g_ref.at[:, 1, y1, half_b], yp, ym
-    )
-    far_e.pass_on()
-    last_z += [over_z(g_ref.at[x3, z, :, late_a]), over_z(g_ref.at[x1, z, :, late_a])]
-    far_f.pass_on()
-    last_z += [over_z(g_ref.at[:, z, y3, late_b]), over_z(g_ref.at[:, z, y1, late_b])]
-    far_e.arrive()
-    last_z.append(over_z(g_ref.at[x2, z, :, late_a]))
-    far_f.arrive()
-    last_z.append(over_z(g_ref.at[:, z, y2, late_b]))
-    far_a.pass_on()
-    far_b.pass_on()
-    far_a.arrive()
-    far_b.arrive()
-    for copy in last_z:
-        copy.wait_recv()
-    for copy in [first_z] + last_z:
+        return lost
+
+    x1, x3 = lax.rem(x + 1, 4), lax.rem(x + 3, 4)
+    y1, y3 = lax.rem(y + 1, 4), lax.rem(y + 3, 4)
+
+    def rows_of(b):
+        return pl.ds(b * 128, 128), pl.ds((2 + b) * 128, 128)
+
+    def over_z(b):
+        return [
+            copies.start(g_ref.at[x, z, y, rows], g_ref.at[x, z, y, rows], zp) for rows in rows_of(b)
+        ]
+
+    def near(b, sent):
+        ra, rb = rows_of(b)
+        sent[0].wait_recv()
+        ring_a = RingGather(
+            copies, g_ref.at[x, :, y, ra], g_ref.at[x, 0, y3, ra], g_ref.at[x, 1, y1, ra], yp, ym
+        )
+        sent[1].wait_recv()
+        ring_b = RingGather(
+            copies, g_ref.at[x, :, y, rb], g_ref.at[x3, 0, y, rb], g_ref.at[x1, 1, y, rb], xp, xm
+        )
+        return ring_a, ring_b
+
+    def far(b, rings):
+        ra, rb = rows_of(b)
+        rings[0].arrive()
+        ring_a = RingGather(
+            copies, g_ref.at[x, :, :, ra], g_ref.at[x3, 0, :, ra], g_ref.at[x1, 1, :, ra], xp, xm
+        )
+        rings[1].arrive()
+        ring_b = RingGather(
+            copies, g_ref.at[:, :, y, rb], g_ref.at[:, 0, y3, rb], g_ref.at[:, 1, y1, rb], yp, ym
+        )
+        return ring_a, ring_b
+
+    def pass_on(rings):
+        for ring in rings:
+            ring.pass_on()
+
+    each(first[0], "code_far")
+    pl.semaphore_wait(barrier, 5)
+    each(first[0], "send_far")
+    each(first[0], "send_near")
+    start(first[1])
+    each(first[0], "pass_on")
+    arrive(first[0])
+    start(second[0])
+    each(first[1], "pass_on")
+    each(second[0], "pass_on")
+    arrive(first[1])
+    start(second[1])
+    arrive(second[0])
+    pair_0 = pair_up(0)
+    each(second[1], "pass_on")
+    pair_0.wait()
+    lost = owner(0, jnp.zeros((1, 128), F32))
+    z_0 = over_z(0)
+    arrive(second[1])
+    pair_1 = pair_up(1)
+    near_0 = near(0, z_0)
+    pair_1.wait()
+    bsum_ref[...] = owner(1, lost)
+    z_1 = over_z(1)
+    pass_on(near_0)
+    near_1 = near(1, z_1)
+    far_0 = far(0, near_0)
+    pass_on(near_1)
+    far_1 = far(1, near_1)
+    pass_on(far_0)
+    pass_on(far_1)
+    arrive(far_0)
+    arrive(far_1)
+    for copy in z_0 + z_1:
         copy.wait_send()
-    for ring in (near_a, near_b, near_e, near_f, far_a, far_b, far_e, far_f):
-        ring.drain()
+    for rings in first + second + [near_0, near_1, far_0, far_1]:
+        for ring in rings:
+            ring.drain()
 
 
 def reduce_gather(totals, bias, cotangent):
     vmem = pl.BlockSpec(memory_space=pltpu.VMEM)
-
-    def ring(half):
-        return [
-            pltpu.VMEM((12,) + half, jnp.int16),
-            pltpu.VMEM((12, 8, 128), F32),
-            pltpu.VMEM((2,) + half, F32),
-        ]
-
     return pl.pallas_call(
         reduce_gather_kernel,
         out_shape=(
@@ -466,12 +513,15 @@
         ),
         in_specs=[vmem] * 3,
         out_specs=(vmem,) * 3,
-        scratch_shapes=ring((4, 256, 128)) * 2
-        + ring((256, 128)) * 2
-        + [
-            pltpu.VMEM((2, 256, 128), F32),
-            pltpu.SemaphoreType.DMA((92,)),
-            pltpu.SemaphoreType.DMA((92,)),
+        scratch_shapes=[
+            pltpu.VMEM((4, 12, 4, 128, 128), jnp.int16),
+            pltpu.VMEM((4, 12, 8, 128), F32),
+            pltpu.VMEM((4, 12, 128, 128), jnp.int16),
+            pltpu.VMEM((4, 12, 8, 128), F32),
+            pltpu.VMEM((2, 2, 2, 128, 128), F32),
+            pltpu.VMEM((2, 2, 128, 128), F32),
+            pltpu.SemaphoreType.DMA((140,)),
+            pltpu.SemaphoreType.DMA((140,)),
         ],
         compiler_params=pltpu.CompilerParams(
             collective_id=0, has_side_effects=True, vmem_limit_bytes=REDUCE_VMEM
@@ -487,35 +537,27 @@
 ):
     here = place()
     x, z, y, h, k = here
-    mine, line = x * 4 + y, (h * 2 + k) * 2 + z
+    mine, line = x * 4 + y, h * 2 + z
     plane = [
         (shifted(here, dx=dx, dy=dy), lax.rem(x + dx, 4) * 4 + lax.rem(y + dy, 4))
         for dx in range(4)
         for dy in range(4)
         if (dx, dy) != (0, 0)
     ]
-    column = [
-        shifted(here, dz=dz, dh=dh, dk=dk)
-        for dh in range(4)
-        for dz in range(2)
-        for dk in range(2)
-        if (dz, dh, dk) != (0, 0, 0)
-    ]
+    column = [shifted(here, dz=dz, dh=dh) for dh in range(4) for dz in range(2) if (dz, dh) != (0, 0)]
+    partner = shifted(here, dk=1)
     barrier = pltpu.get_barrier_semaphore()
-    for peer in column + [p for p, _ in plane]:
+    for peer in [partner] + column + [p for p, _ in plane]:
         pl.semaphore_signal(barrier, inc=1, device_id=peer, device_id_type=MESH)
     lost[...] = jnp.concatenate([bsum_ref[...], jnp.zeros((7, 128), F32)], axis=0)
-    pl.semaphore_wait(barrier, 30)
+    pl.semaphore_wait(barrier, 23)
     copies = Copies(send, recv)
 
     other = 1 - k
-    partner = shifted(here, dk=1)
     pairs = {}
     for dh in (2, 1, 3, 0):
         to = lax.rem(h + dh, 4)
         pairs[dh] = copies.start(t_ref.at[to, other], from_core.at[to], partner)
-    bias_plane = [copies.start(lost, plane_lost.at[mine], p) for p, _ in plane]
-    plane_lost[mine] = lost[...]
     above, below = shifted(here, dh=1), shifted(here, dh=3)
     chips = []
 
@@ -535,16 +577,21 @@
     send(both(1, lower), 2, above)
     pairs[3].wait_recv()
     send(both(3, upper), 3, below)
-    for copy in bias_plane:
-        copy.wait_recv()
-    total_lost[...] = sum_of(plane_lost)
-    bias_line = [copies.start(total_lost, line_lost.at[line], p) for p in column]
-    line_lost[line] = total_lost[...]
     pairs[0].wait_recv()
+    bias_plane = [copies.start(lost, plane_lost.at[mine], p) for p, _ in plane]
+    plane_lost[mine] = lost[...]
     chips[0].wait_recv()
     send(both(1, upper) + from_chip[0].astype(F32), 4, above)
     chips[1].wait_recv()
     send(both(3, lower) + from_chip[1].astype(F32), 5, below)
+    for copy in bias_plane:
+        copy.wait_recv()
+    total_lost[0] = sum_of(plane_lost)
+    bias_line = [copies.start(total_lost.at[0], total_lost.at[1], partner)]
+    bias_line[0].wait_recv()
+    total_lost[2] = total_lost[0] + total_lost[1]
+    bias_line += [copies.start(total_lost.at[2], line_lost.at[line], p) for p in column]
+    line_lost[line] = total_lost[2]
     for copy in chips[2:]:
         copy.wait_recv()
     own = jnp.concatenate(
@@ -568,15 +615,18 @@
         grad, weight_ref[...], (((1,), (1,)), ((), ())), preferred_element_type=F32
     ).astype(BF16)
     scale = 131072.0**-0.5
-    for copy in bias_line:
+    for copy in bias_line[1:]:
         copy.wait_recv()
     gb_ref[...] = sum_of(line_lost)[0:1] * scale
     for copy in sent:
         copy.wait_recv()
-    total[...] = sum_of(plane_parts)
-    spread = [copies.start(total, line_parts.at[line], p) for p in column]
-    line_parts[line] = total[...]
-    for copy in spread:
+    total[0] = sum_of(plane_parts)
+    spread = [copies.start(total.at[0], total.at[1], partner)]
+    spread[0].wait_recv()
+    total[2] = total[0] + total[1]
+    spread += [copies.start(total.at[2], line_parts.at[line], p) for p in column]
+    line_parts[line] = total[2]
+    for copy in spread[1:]:
         copy.wait_recv()
     whole[rows(mine)] = sum_of(line_parts) * scale
     back = [copies.start(whole.at[rows(mine)], whole.at[rows(mine)], p) for p, _ in plane]
@@ -598,8 +648,8 @@
     vmem = pl.BlockSpec(memory_space=pltpu.VMEM)
     sums = [
         pltpu.VMEM((16, 8, 128), F32),
-        pltpu.VMEM((8, 128), F32),
-        pltpu.VMEM((16, 8, 128), F32),
+        pltpu.VMEM((3, 8, 128), F32),
+        pltpu.VMEM((8, 8, 128), F32),
     ]
     return pl.pallas_call(
         finish_kernel,

time: 142 us -> 139 us (0.979)
  Pallas kernels: 139 us -> 136 us
    pallas_call x1, Pallas kernels: 68.3 us -> 65.9 us  [reduce_gather(): pl.pallas_call(reduce_gather_kernel, out_shape=(jax.ShapeDtypeStruct((512...]
where the time goes in v6:
time: 139 us
  Pallas kernels  136 us (98%)
  local copies, waits for them, and re-layouts  1.82 us (1%)
    pallas_call x1, Pallas kernels, reduce_gather(): pl.pallas_call(reduce_gather_kernel, out_shape=(jax.ShapeDtypeStruct((512...  65.9 us
    pallas_call x1, Pallas kernels, finish(): pl.pallas_call(finish_kernel, out_shape=(jax.ShapeDtypeStruct((512, 128),...  45 us
    pallas_call x1, Pallas kernels, prepare(): pl.pallas_call(prepare_kernel, out_shape=(jax.ShapeDtypeStruct((slots, 12...  21.3 us

profile of v6, /device:TPU:1, one launch (start us, length us, event | category | flops | bytes accessed | tf_op | source)
XLA Modules:
  0.0 139.1 jit_solution(14581508995801020291)
XLA Ops:
  1.3 21.3 %prepare.1 = (bf16[512,128,128]{2,1,0:T(8,128)(2,1)S(1)}, bf16[8,4,128,128]{3,2,1,0:T(8,128)(2,1)S(1)}) custom-call(s32[1,1]{1,0:T(1,128)S(6)} %copy.16.count_ref, s32[1,1,512,128]{3,2,1,0:T(8,128)} %off_hbm.1, bf16[1,1,512,128]{3,2,1,0:T(8,128)(2,1)} %w_hbm.1, bf16[512,128]{1,0:T(8,128)(2,1)} %feat_ref.1, bf16[128,128]{1,0:T(8,128)(2,1)} %weight_ref.1), custom_call_target="tpu_custom_call" | custom-call | tf_op jit(solution)/shard_map/prepare/pallas_call | solution.py:163
  22.5 0.0 copy-start.1
  22.6 0.0 copy-start.3
  22.6 1.9 %forward.1 = f32[128,128,128]{2,1,0:T(8,128)S(1)} custom-call(s32[1,1]{1,0:T(1,128)S(6)} %copy.16.count_ref, s32[1,1,512]{2,1,0:T(1,128)} %row_hbm.3, s32[1,1,512]{2,1,0:T(1,128)} %col_hbm.3, bf16[512,128,128]{2,1,0:T(8,128)(2,1)S(1)} %get-tuple-element.14.d_ref, bf16[32,128,128]{2,1,0:T(8,128)(2,1)S(1)} %bitcast.9), custom_call_target="tpu_custom_call" | custom-call | tf_op jit(solution)/shard_map/forward/pallas_call | solution.py:250
  24.5 0.0 copy-done.1
  24.5 0.0 copy-done.3
  24.5 65.9 %reduce_gather.1 = (bf16[512,128]{1,0:T(8,128)(2,1)S(1)}, bf16[4,2,4,512,128]{4,3,2,1,0:T(8,128)(2,1)S(1)}, f32[1,128]{1,0:T(1,128)S(1)}) custom-call(f32[4,2,4,512,128]{4,3,2,1,0:T(8,128)S(1)} %bitcast.6, f32[1,128]{1,0:T(1,128)S(1)} %bitcast.10, bf16[512,128]{1,0:T(8,128)(2,1)S(1)} %copy-done.1), custom_call_target="tpu_custom_call" | custom-call | tf_op jit(solution)/shard_map/reduce_gather/pallas_call | solution.py:507
  90.4 0.0 copy-start
  90.4 0.0 copy-start.2
  90.4 1.8 %backward.1 = (f32[32,128,128]{2,1,0:T(8,128)S(1)}, bf16[512,128]{1,0:T(8,128)(2,1)}) custom-call(s32[1,1]{1,0:T(1,128)S(6)} %copy.16.count_ref, s32[1,1,512]{2,1,0:T(1,128)} %row_hbm.3, s32[1,1,512]{2,1,0:T(1,128)} %col_hbm.3, bf16[512,128,128]{2,1,0:T(8,128)(2,1)S(1)} %get-tuple-element.14.d_ref, bf16[128,128,128]{2,1,0:T(8,128)(2,1)S(1)} %bitcast.7, ...), custom_call_target="tpu_custom_call" | custom-call | tf_op jit(solution)/shard_map/backward/pallas_call | solution.py:259
  92.2 0.0 copy-done
  92.2 0.0 copy-done.2
  92.2 45.0 %finish.1 = (bf16[512,128]{1,0:T(8,128)(2,1)S(1)}, f32[128,128]{1,0:T(8,128)S(1)}, f32[1,128]{1,0:T(1,128)S(1)}) custom-call(f32[4,2,512,128]{3,2,1,0:T(8,128)S(1)} %bitcast.8, bf16[512,128]{1,0:T(8,128)(2,1)S(1)} %copy-done, bf16[128,128]{1,0:T(8,128)(2,1)S(1)} %copy-done.2, f32[1,128]{1,0:T(1,128)S(1)} %get-tuple-element.20.bsum_ref), custom_call_target="tpu_custom_call" | custom-call | tf_op jit(solution)/shard_map/finish/pallas_call | solution.py:654
  137.3 0.7 copy.17
  137.9 0.6 copy.18
  138.5 0.5 copy.19
Async XLA Ops:
  22.5 1.9 %copy-start.1 = (bf16[512,128]{1,0:T(8,128)(2,1)S(1)}, bf16[512,128]{1,0:T(8,128)(2,1)}, u32[]{:S(2)}) copy-start(bf16[512,128]{1,0:T(8,128)(2,1)} %cot_ref.1) | copy-start | bytes 393220
  22.6 1.9 %copy-start.3 = (f32[128]{0:T(128)S(1)}, f32[128]{0:T(128)}, u32[]{:S(2)}) copy-start(f32[128]{0:T(128)} %param.11) | copy-start | bytes 1540
  90.4 1.8 %copy-start = (bf16[512,128]{1,0:T(8,128)(2,1)S(1)}, bf16[512,128]{1,0:T(8,128)(2,1)}, u32[]{:S(2)}) copy-start(bf16[512,128]{1,0:T(8,128)(2,1)} %feat_ref.1) | copy-start | bytes 393220
  90.4 1.8 %copy-start.2 = (bf16[128,128]{1,0:T(8,128)(2,1)S(1)}, bf16[128,128]{1,0:T(8,128)(2,1)}, u32[]{:S(2)}) copy-start(bf16[128,128]{1,0:T(8,128)(2,1)} %weight_ref.1) | copy-start | bytes 98308

commit v7 on v6

--- a/solution.py
+++ b/solution.py
@@ -1,4 +1,4 @@
-import functools
+import math
 
 import jax
 import jax.numpy as jnp
@@ -11,6 +11,7 @@
 F32 = jnp.float32
 BF16 = jnp.bfloat16
 BATCH = 64
+SUM_BATCH = 128
 PREP_VMEM = 4 << 20
 SUMS_VMEM = 4 << 20
 REDUCE_VMEM = 16 << 20
@@ -205,13 +206,13 @@
         copy.wait()
 
     def step(i, carry):
-        for s in range(BATCH):
-            n = i * BATCH + s
+        for s in range(SUM_BATCH):
+            n = i * SUM_BATCH + s
             r, c = row_ref[0, 0, n], col_ref[0, 0, n]
             t_ref[r] += jnp.dot(x_ref[c], d_ref[n], preferred_element_type=F32)
         return carry
 
-    lax.fori_loop(0, lax.div(count_ref[0, 0] + (BATCH - 1), BATCH), step, 0)
+    lax.fori_loop(0, lax.div(count_ref[0, 0] + (SUM_BATCH - 1), SUM_BATCH), step, 0)
 
 
 def backward_kernel(
@@ -225,13 +226,13 @@
         copy.wait()
 
     def step(i, carry):
-        for s in range(BATCH):
-            n = i * BATCH + s
+        for s in range(SUM_BATCH):
+            n = i * SUM_BATCH + s
             r, c = row_ref[0, 0, n], col_ref[0, 0, n]
             t_ref[c] += jnp.dot(d_ref[n], y_ref[r], preferred_element_type=F32)
         return carry
 
-    lax.fori_loop(0, lax.div(count_ref[0, 0] + (BATCH - 1), BATCH), step, 0)
+    lax.fori_loop(0, lax.div(count_ref[0, 0] + (SUM_BATCH - 1), SUM_BATCH), step, 0)
     passed.wait()
 
 
@@ -268,51 +269,53 @@
 
 
 LEVELS = 32766.0
-
-
-def blocks_of(ref):
-    if len(ref.shape) == 2:
-        return [(Ellipsis,)]
-    return [(i, Ellipsis) for i in range(ref.shape[0])]
-
-
-def encode(value, at, n, q_ref, s_ref):
+STEPS = 64.0 / math.log(2.0)
+
+
+def block_rows_of(n):
+    return pl.ds(n * 128 if isinstance(n, int) else pl.multiple_of(n * 128, 128), 128)
+
+
+def encode(value, n, q_ref):
     size = jnp.abs(value)
     most = jnp.maximum(jnp.max(size, axis=0, keepdims=True), 1e-30)
-    level = jnp.sqrt(size * (1.0 / most)) * LEVELS + 0.5
-    q_ref[at] = jnp.where(value < 0, -level, level).astype(jnp.int32).astype(jnp.int16)
-    s_ref[n : n + 1] = most * (1.0 / (LEVELS * LEVELS))
-
-
-def decode(at, n, q_ref, s_ref):
-    level = q_ref[at].astype(jnp.int32).astype(F32)
+    step = jnp.ceil(jnp.log(most) * STEPS)
+    level = jnp.sqrt(size * jnp.exp(step * (-1.0 / STEPS))) * LEVELS + 0.5
+    q_ref[block_rows_of(n)] = jnp.where(value < 0, -level, level).astype(jnp.int32).astype(jnp.int16)
+    return step
+
+
+def decode(n, q_ref, s_ref):
+    level = q_ref[block_rows_of(n)].astype(jnp.int32).astype(F32)
     return level * jnp.abs(level) * s_ref[pl.ds(n, 1)]
 
 
 class RingSum:
-    def __init__(self, copies, value, me, plus, minus, q, scales):
+    def __init__(self, copies, value, me, plus, minus, q, scales, blocks):
+        self.blocks = blocks
         self.copies, self.value, self.q, self.scales = copies, value, q, scales
         self.me, self.p1, self.p2, self.p3 = me, lax.rem(me + 1, 4), lax.rem(me + 2, 4), lax.rem(me + 3, 4)
         self.plus, self.minus = plus, minus
         self.sent = {}
 
     def code(self, value, slot):
-        for n, at in enumerate(blocks_of(self.q.at[slot])):
-            encode(value(n, at), at, n, self.q.at[slot], self.scales.at[slot])
+        q = self.q.at[slot]
+        steps = [encode(value(n, at), n, q) for n, at in enumerate(self.blocks)]
+        steps.append(jnp.zeros((16 - len(steps), 128), F32))
+        tail = jnp.concatenate(steps, axis=0)
+        q[pl.ds(len(self.blocks) * 128, 16)] = tail.astype(jnp.int32).astype(jnp.int16)
 
     def start(self, slot, device):
-        self.sent[slot] = (
-            self.copies.start(self.q.at[slot], self.q.at[slot + 6], device),
-            self.copies.start(self.scales.at[slot], self.scales.at[slot + 6], device),
-        )
-
-    def got(self, slot, n, at):
-        return decode(at, n, self.q.at[slot + 6], self.scales.at[slot + 6])
+        self.sent[slot] = self.copies.start(self.q.at[slot], self.q.at[slot + 6], device)
+
+    def got(self, slot, n):
+        return decode(n, self.q.at[slot + 6], self.scales.at[slot])
 
     def wait(self, *slots):
         for slot in slots:
-            for copy in self.sent[slot]:
-                copy.wait_recv()
+            self.sent[slot].wait_recv()
+            tail = self.q[slot + 6, pl.ds(len(self.blocks) * 128, 16)].astype(jnp.int32).astype(F32)
+            self.scales[slot] = jnp.exp(tail * (1.0 / STEPS)) * (1.0 / (LEVELS * LEVELS))
 
     def code_far(self, half):
         self.code(self.value(self.p2, half), half)
@@ -327,7 +330,7 @@
     def pass_on(self, half):
         self.wait(half)
         own = self.value((self.p1, self.p3)[half], half)
-        self.code(lambda n, at: own(n, at) + self.got(half, n, at), half + 4)
+        self.code(lambda n, at: own(n, at) + self.got(half, n), half + 4)
         self.start(half + 4, (self.plus, self.minus)[half])
 
     def arrive(self):
@@ -336,14 +339,13 @@
     def total(self, half, n, at):
         return (
             self.value(self.me, half)(n, at)
-            + self.got(3 - half, n, at)
-            + self.got(half + 4, n, at)
+            + self.got(3 - half, n)
+            + self.got(half + 4, n)
         )
 
     def drain(self):
-        for pair in self.sent.values():
-            for copy in pair:
-                copy.wait_send()
+        for copy in self.sent.values():
+            copy.wait_send()
 
 
 def reduce_gather_kernel(
@@ -360,11 +362,13 @@
         pl.semaphore_signal(barrier, inc=1, device_id=peer, device_id_type=MESH)
     copies = Copies(send, recv)
 
-    def ring_over_x(number, q, scale, value):
-        return RingSum(copies, value, x, xp, xm, q.at[number], scale.at[number])
-
-    def ring_over_y(number, q, scale, value):
-        return RingSum(copies, value, y, yp, ym, q.at[number], scale.at[number])
+    four, one = [(i, Ellipsis) for i in range(4)], [(Ellipsis,)]
+
+    def ring_over_x(number, q, scale, blocks, value):
+        return RingSum(copies, value, x, xp, xm, q.at[number], scale.at[number], blocks)
+
+    def ring_over_y(number, q, scale, blocks, value):
+        return RingSum(copies, value, y, yp, ym, q.at[number], scale.at[number], blocks)
 
     def part_a(b):
         rows = slice(b * 128, (b + 1) * 128)
@@ -379,13 +383,13 @@
 
     first, second = [], []
     for b in range(2):
-        over_x = ring_over_x(2 * b, first_q, first_scale, part_a(b))
-        over_y = ring_over_y(2 * b + 1, first_q, first_scale, part_b(b))
+        over_x = ring_over_x(2 * b, first_q, first_scale, four, part_a(b))
+        over_y = ring_over_y(2 * b + 1, first_q, first_scale, four, part_b(b))
         first.append((over_x, over_y))
         second.append(
             (
-                ring_over_y(2 * b, second_q, second_scale, then(over_x)),
-                ring_over_x(2 * b + 1, second_q, second_scale, then(over_y)),
+                ring_over_y(2 * b, second_q, second_scale, one, then(over_x)),
+                ring_over_x(2 * b + 1, second_q, second_scale, one, then(over_y)),
             )
         )
 
@@ -514,14 +518,14 @@
         in_specs=[vmem] * 3,
         out_specs=(vmem,) * 3,
         scratch_shapes=[
-            pltpu.VMEM((4, 12, 4, 128, 128), jnp.int16),
-            pltpu.VMEM((4, 12, 8, 128), F32),
-            pltpu.VMEM((4, 12, 128, 128), jnp.int16),
-            pltpu.VMEM((4, 12, 8, 128), F32),
+            pltpu.VMEM((4, 12, 4 * 128 + 16, 128), jnp.int16),
+            pltpu.VMEM((4, 6, 16, 128), F32),
+            pltpu.VMEM((4, 12, 128 + 16, 128), jnp.int16),
+            pltpu.VMEM((4, 6, 16, 128), F32),
             pltpu.VMEM((2, 2, 2, 128, 128), F32),
             pltpu.VMEM((2, 2, 128, 128), F32),
-            pltpu.SemaphoreType.DMA((140,)),
-            pltpu.SemaphoreType.DMA((140,)),
+            pltpu.SemaphoreType.DMA((90,)),
+            pltpu.SemaphoreType.DMA((90,)),
         ],
         compiler_params=pltpu.CompilerParams(
             collective_id=0, has_side_effects=True, vmem_limit_bytes=REDUCE_VMEM
@@ -679,6 +683,31 @@
     )(partial, features, weight, bias_sum)
 
 
+def export_kernel(*refs):
+    count = len(refs) // 2
+    sem = refs[-1]
+    copies = [
+        pltpu.make_async_copy(refs[i], refs[count + i], sem.at[i]) for i in range(count)
+    ]
+    for copy in copies:
+        copy.start()
+    for copy in copies:
+        copy.wait()
+
+
+def export(*arrays):
+    vmem, hbm = pl.BlockSpec(memory_space=pltpu.VMEM), pl.BlockSpec(memory_space=pltpu.HBM)
+    return pl.pallas_call(
+        export_kernel,
+        in_specs=[vmem] * len(arrays),
+        out_specs=(hbm,) * len(arrays),
+        out_shape=tuple(jax.ShapeDtypeStruct(a.shape, a.dtype) for a in arrays),
+        scratch_shapes=[pltpu.SemaphoreType.DMA((len(arrays),))],
+        compiler_params=pltpu.CompilerParams(vmem_limit_bytes=1 << 20),
+        name="export",
+    )(*arrays)
+
+
 def shards(
     features, weight, bias, cotangent, block_count, block_rows, block_cols, edge_offsets, edge_weight
 ):
@@ -691,8 +720,8 @@
     partial, output = block_sums(
         "backward", *tables, dense, grads.reshape(128, 128, 128), 32, output
     )
-    grad_features, grad_weight, grad_bias = finish(
-        partial.reshape(4, 2, 512, 128), features, weight, bias_sum
+    grad_features, grad_weight, grad_bias = export(
+        *finish(partial.reshape(4, 2, 512, 128), features, weight, bias_sum)
     )
     return (output, grad_features, grad_weight, grad_bias.reshape(128))
 

time: 139 us -> 137 us (0.986)
  local copies, waits for them, and re-layouts: 1.82 us -> 0.03 us
    pallas_call x1, Pallas kernels: 45 us -> 38.1 us  [finish(): pl.pallas_call(finish_kernel, out_shape=(jax.ShapeDtypeStruct((512, 128),...]
    pallas_call x1, Pallas kernels: 1.77 us -> 7.56 us  [block_sums(): pl.pallas_call(backward_kernel, in_specs=[smem, hbm, hbm] + [vmem] * 3, o...]
    pallas_call x1, Pallas kernels: 65.9 us -> 60.2 us  [reduce_gather(): pl.pallas_call(reduce_gather_kernel, out_shape=(jax.ShapeDtypeStruct((512...]
    pallas_call x1, Pallas kernels: 1.9 us -> 7.2 us  [block_sums(): pl.pallas_call(forward_kernel, in_specs=[smem, hbm, hbm] + [vmem] * 2, ou...]
    unnamed x11 -> x8, local copies, waits for them, and re-layouts: 1.82 us -> 0.03 us
where the time goes in v7:
time: 137 us
  Pallas kernels  135 us (99%)
  between operations  1.54 us (1%)
    pallas_call x1, Pallas kernels, reduce_gather(): pl.pallas_call(reduce_gather_kernel, out_shape=(jax.ShapeDtypeStruct((512...  60.2 us
    pallas_call x1, Pallas kernels, finish(): pl.pallas_call(finish_kernel, out_shape=(jax.ShapeDtypeStruct((512, 128),...  38.1 us
    pallas_call x1, Pallas kernels, prepare(): pl.pallas_call(prepare_kernel, out_shape=(jax.ShapeDtypeStruct((slots, 12...  21.3 us
    pallas_call x1, Pallas kernels, block_sums(): pl.pallas_call(backward_kernel, in_specs=[smem, hbm, hbm] + [vmem] * 3, o...  7.56 us
    pallas_call x1, Pallas kernels, block_sums(): pl.pallas_call(forward_kernel, in_specs=[smem, hbm, hbm] + [vmem] * 2, ou...  7.2 us

profile of v7, /device:TPU:1, one launch (start us, length us, event | category | flops | bytes accessed | tf_op | source)
XLA Modules:
  0.0 136.6 jit_solution(4304761311490340351)
XLA Ops:
  1.3 21.3 %prepare.1 = (bf16[512,128,128]{2,1,0:T(8,128)(2,1)S(1)}, bf16[8,4,128,128]{3,2,1,0:T(8,128)(2,1)S(1)}) custom-call(s32[1,1]{1,0:T(1,128)S(6)} %copy.13.count_ref, s32[1,1,512,128]{3,2,1,0:T(8,128)} %off_hbm.1, bf16[1,1,512,128]{3,2,1,0:T(8,128)(2,1)} %w_hbm.1, bf16[512,128]{1,0:T(8,128)(2,1)} %feat_ref.1, bf16[128,128]{1,0:T(8,128)(2,1)} %weight_ref.1), custom_call_target="tpu_custom_call" | custom-call | tf_op jit(solution)/shard_map/prepare/pallas_call | solution.py:164
  22.5 0.0 copy-start.1
  22.6 0.0 copy-start.3
  22.6 7.2 %forward.1 = f32[128,128,128]{2,1,0:T(8,128)S(1)} custom-call(s32[1,1]{1,0:T(1,128)S(6)} %copy.13.count_ref, s32[1,1,512]{2,1,0:T(1,128)} %row_hbm.3, s32[1,1,512]{2,1,0:T(1,128)} %col_hbm.3, bf16[512,128,128]{2,1,0:T(8,128)(2,1)S(1)} %get-tuple-element.17.d_ref, bf16[32,128,128]{2,1,0:T(8,128)(2,1)S(1)} %bitcast.9), custom_call_target="tpu_custom_call" | custom-call | tf_op jit(solution)/shard_map/forward/pallas_call | solution.py:251
  29.8 0.0 copy-done.1
  29.8 0.0 copy-done.3
  29.8 60.2 %reduce_gather.1 = (bf16[512,128]{1,0:T(8,128)(2,1)S(1)}, bf16[4,2,4,512,128]{4,3,2,1,0:T(8,128)(2,1)S(1)}, f32[1,128]{1,0:T(1,128)S(1)}) custom-call(f32[4,2,4,512,128]{4,3,2,1,0:T(8,128)S(1)} %bitcast.6, f32[1,128]{1,0:T(1,128)S(1)} %bitcast.10, bf16[512,128]{1,0:T(8,128)(2,1)S(1)} %copy-done.1), custom_call_target="tpu_custom_call" | custom-call | tf_op jit(solution)/shard_map/reduce_gather/pallas_call | solution.py:511
  90.0 0.0 copy-start
  90.0 0.0 copy-start.2
  90.1 7.6 %backward.1 = (f32[32,128,128]{2,1,0:T(8,128)S(1)}, bf16[512,128]{1,0:T(8,128)(2,1)}) custom-call(s32[1,1]{1,0:T(1,128)S(6)} %copy.13.count_ref, s32[1,1,512]{2,1,0:T(1,128)} %row_hbm.3, s32[1,1,512]{2,1,0:T(1,128)} %col_hbm.3, bf16[512,128,128]{2,1,0:T(8,128)(2,1)S(1)} %get-tuple-element.17.d_ref, bf16[128,128,128]{2,1,0:T(8,128)(2,1)S(1)} %bitcast.7, ...), custom_call_target="tpu_custom_call" | custom-call | tf_op jit(solution)/shard_map/backward/pallas_call | solution.py:260
  97.6 0.0 copy-done
  97.6 0.0 copy-done.2
  97.6 38.1 %finish.1 = (bf16[512,128]{1,0:T(8,128)(2,1)S(1)}, f32[128,128]{1,0:T(8,128)S(1)}, f32[1,128]{1,0:T(1,128)S(1)}) custom-call(f32[4,2,512,128]{3,2,1,0:T(8,128)S(1)} %bitcast.8, bf16[512,128]{1,0:T(8,128)(2,1)S(1)} %copy-done, bf16[128,128]{1,0:T(8,128)(2,1)S(1)} %copy-done.2, f32[1,128]{1,0:T(1,128)S(1)} %get-tuple-element.23.bsum_ref), custom_call_target="tpu_custom_call" | custom-call | tf_op jit(solution)/shard_map/finish/pallas_call | solution.py:658
  135.8 0.7 export.1
Async XLA Ops:
  22.5 7.2 %copy-start.1 = (bf16[512,128]{1,0:T(8,128)(2,1)S(1)}, bf16[512,128]{1,0:T(8,128)(2,1)}, u32[]{:S(2)}) copy-start(bf16[512,128]{1,0:T(8,128)(2,1)} %cot_ref.1) | copy-start | bytes 393220
  22.6 7.2 %copy-start.3 = (f32[128]{0:T(128)S(1)}, f32[128]{0:T(128)}, u32[]{:S(2)}) copy-start(f32[128]{0:T(128)} %param.11) | copy-start | bytes 1540
  90.0 7.6 %copy-start = (bf16[512,128]{1,0:T(8,128)(2,1)S(1)}, bf16[512,128]{1,0:T(8,128)(2,1)}, u32[]{:S(2)}) copy-start(bf16[512,128]{1,0:T(8,128)(2,1)} %feat_ref.1) | copy-start | bytes 393220
  90.0 7.6 %copy-start.2 = (bf16[128,128]{1,0:T(8,128)(2,1)S(1)}, bf16[128,128]{1,0:T(8,128)(2,1)}, u32[]{:S(2)}) copy-start(bf16[128,128]{1,0:T(8,128)(2,1)} %weight_ref.1) | copy-start | bytes 98308

commit v8 on v7

--- a/solution.py
+++ b/solution.py
@@ -427,11 +427,61 @@
             g_ref[x, z, y, rows] = grad.astype(BF16)
         return lost
 
-    x1, x3 = lax.rem(x + 1, 4), lax.rem(x + 3, 4)
-    y1, y3 = lax.rem(y + 1, 4), lax.rem(y + 3, 4)
+    x1, x2, x3 = (lax.rem(x + i, 4) for i in (1, 2, 3))
+    y1, y2, y3 = (lax.rem(y + i, 4) for i in (1, 2, 3))
 
     def rows_of(b):
-        return pl.ds(b * 128, 128), pl.ds((2 + b) * 128, 128)
+        size = 128 if b else 64
+        return pl.ds(b * 128, size), pl.ds((2 + b) * 128, size)
+
+    def late_rows(start=0, size=64):
+        return pl.ds(64 + start, size), pl.ds(256 + 64 + start, size)
+
+    def late_near():
+        (re, rf), (re0, rf0), (re1, rf1) = late_rows(), late_rows(0, 32), late_rows(32, 32)
+        return (
+            RingGather(
+                copies, g_ref.at[x, z, y, re], g_ref.at[x, z, y3, re0], g_ref.at[x, z, y1, re1], yp, ym
+            ),
+            RingGather(
+                copies, g_ref.at[x, z, y, rf], g_ref.at[x3, z, y, rf0], g_ref.at[x1, z, y, rf1], xp, xm
+            ),
+        )
+
+    late_z = []
+
+    def late_over_z(ref):
+        late_z.append(copies.start(ref, ref, zp))
+
+    def late_far(rings):
+        re, rf = late_rows()
+        rings[0].arrive()
+        ring_e = RingGather(
+            copies, g_ref.at[x, z, :, re], g_ref.at[x3, z, 0:2, re], g_ref.at[x1, z, 2:4, re], xp, xm
+        )
+        late_over_z(g_ref.at[x, z, :, re])
+        rings[1].arrive()
+        ring_f = RingGather(
+            copies, g_ref.at[:, z, y, rf], g_ref.at[0:2, z, y3, rf], g_ref.at[2:4, z, y1, rf], yp, ym
+        )
+        late_over_z(g_ref.at[:, z, y, rf])
+        return ring_e, ring_f
+
+    def late_pass_on(rings):
+        re, rf = late_rows()
+        rings[0].pass_on()
+        late_over_z(g_ref.at[x3, z, :, re])
+        late_over_z(g_ref.at[x1, z, :, re])
+        rings[1].pass_on()
+        late_over_z(g_ref.at[:, z, y3, rf])
+        late_over_z(g_ref.at[:, z, y1, rf])
+
+    def late_arrive(rings):
+        re, rf = late_rows()
+        rings[0].arrive()
+        late_over_z(g_ref.at[x2, z, :, re])
+        rings[1].arrive()
+        late_over_z(g_ref.at[:, z, y2, rf])
 
     def over_z(b):
         return [
@@ -483,25 +533,31 @@
     each(second[1], "pass_on")
     pair_0.wait()
     lost = owner(0, jnp.zeros((1, 128), F32))
-    z_0 = over_z(0)
+    z_0, late = over_z(0), late_near()
     arrive(second[1])
     pair_1 = pair_up(1)
     near_0 = near(0, z_0)
     pair_1.wait()
     bsum_ref[...] = owner(1, lost)
     z_1 = over_z(1)
+    pass_on(late)
     pass_on(near_0)
     near_1 = near(1, z_1)
+    far_late = late_far(late)
     far_0 = far(0, near_0)
     pass_on(near_1)
+    late_pass_on(far_late)
     far_1 = far(1, near_1)
+    late_arrive(far_late)
     pass_on(far_0)
     pass_on(far_1)
     arrive(far_0)
     arrive(far_1)
-    for copy in z_0 + z_1:
+    for copy in late_z:
+        copy.wait_recv()
+    for copy in z_0 + z_1 + late_z:
         copy.wait_send()
-    for rings in first + second + [near_0, near_1, far_0, far_1]:
+    for rings in first + second + [near_0, near_1, far_0, far_1, late, far_late]:
         for ring in rings:
             ring.drain()
 
@@ -524,8 +580,8 @@
             pltpu.VMEM((4, 6, 16, 128), F32),
             pltpu.VMEM((2, 2, 2, 128, 128), F32),
             pltpu.VMEM((2, 2, 128, 128), F32),
-            pltpu.SemaphoreType.DMA((90,)),
-            pltpu.SemaphoreType.DMA((90,)),
+            pltpu.SemaphoreType.DMA((114,)),
+            pltpu.SemaphoreType.DMA((114,)),
         ],
         compiler_params=pltpu.CompilerParams(
             collective_id=0, has_side_effects=True, vmem_limit_bytes=REDUCE_VMEM
@@ -537,7 +593,7 @@
 def finish_kernel(
     t_ref, feat_ref, weight_ref, bsum_ref, gf_ref, gw_ref, gb_ref,
     from_core, outgoing, from_chip, local, plane_parts, total, line_parts, whole,
-    lost, plane_lost, total_lost, line_lost, send, recv,
+    lost, plane_lost, send, recv,
 ):
     here = place()
     x, z, y, h, k = here
@@ -588,14 +644,6 @@
     send(both(1, upper) + from_chip[0].astype(F32), 4, above)
     chips[1].wait_recv()
     send(both(3, lower) + from_chip[1].astype(F32), 5, below)
-    for copy in bias_plane:
-        copy.wait_recv()
-    total_lost[0] = sum_of(plane_lost)
-    bias_line = [copies.start(total_lost.at[0], total_lost.at[1], partner)]
-    bias_line[0].wait_recv()
-    total_lost[2] = total_lost[0] + total_lost[1]
-    bias_line += [copies.start(total_lost.at[2], line_lost.at[line], p) for p in column]
-    line_lost[line] = total_lost[2]
     for copy in chips[2:]:
         copy.wait_recv()
     own = jnp.concatenate(
@@ -619,12 +667,12 @@
         grad, weight_ref[...], (((1,), (1,)), ((), ())), preferred_element_type=F32
     ).astype(BF16)
     scale = 131072.0**-0.5
-    for copy in bias_line[1:]:
+    for copy in bias_plane:
         copy.wait_recv()
-    gb_ref[...] = sum_of(line_lost)[0:1] * scale
+    total[0, 8:16] = sum_of(plane_lost)
     for copy in sent:
         copy.wait_recv()
-    total[0] = sum_of(plane_parts)
+    total[0, 0:8] = sum_of(plane_parts)
     spread = [copies.start(total.at[0], total.at[1], partner)]
     spread[0].wait_recv()
     total[2] = total[0] + total[1]
@@ -632,12 +680,14 @@
     line_parts[line] = total[2]
     for copy in spread[1:]:
         copy.wait_recv()
-    whole[rows(mine)] = sum_of(line_parts) * scale
+    both_sums = sum_of(line_parts) * scale
+    whole[rows(mine)] = both_sums[0:8]
+    gb_ref[...] = both_sums[8:9]
     back = [copies.start(whole.at[rows(mine)], whole.at[rows(mine)], p) for p, _ in plane]
     for copy in back:
         copy.wait_recv()
     gw_ref[...] = whole[...]
-    for copy in [pairs[dh] for dh in range(4)] + bias_plane + chips + bias_line + sent + spread + back:
+    for copy in [pairs[dh] for dh in range(4)] + bias_plane + chips + sent + spread + back:
         copy.wait_send()
 
 
@@ -650,11 +700,6 @@
 
 def finish(partial, features, weight, bias_sum):
     vmem = pl.BlockSpec(memory_space=pltpu.VMEM)
-    sums = [
-        pltpu.VMEM((16, 8, 128), F32),
-        pltpu.VMEM((3, 8, 128), F32),
-        pltpu.VMEM((8, 8, 128), F32),
-    ]
     return pl.pallas_call(
         finish_kernel,
         out_shape=(
@@ -669,12 +714,14 @@
             pltpu.VMEM((6, 256, 128), BF16),
             pltpu.VMEM((6, 256, 128), BF16),
             pltpu.VMEM((128, 128), F32),
-            *sums,
+            pltpu.VMEM((16, 8, 128), F32),
+            pltpu.VMEM((3, 16, 128), F32),
+            pltpu.VMEM((8, 16, 128), F32),
             pltpu.VMEM((128, 128), F32),
             pltpu.VMEM((8, 128), F32),
-            *sums,
-            pltpu.SemaphoreType.DMA((85,)),
-            pltpu.SemaphoreType.DMA((85,)),
+            pltpu.VMEM((16, 8, 128), F32),
+            pltpu.SemaphoreType.DMA((63,)),
+            pltpu.SemaphoreType.DMA((63,)),
         ],
         compiler_params=pltpu.CompilerParams(
             collective_id=1, has_side_effects=True, vmem_limit_bytes=FINISH_VMEM

time: 137 us -> 136 us (level)
    pallas_call x1, Pallas kernels: 38.1 us -> 44.4 us  [finish(): pl.pallas_call(finish_kernel, out_shape=(jax.ShapeDtypeStruct((512, 128),...]
    pallas_call x1, Pallas kernels: 7.56 us -> 2.56 us  [block_sums(): pl.pallas_call(backward_kernel, in_specs=[smem, hbm, hbm] + [vmem] * 3, o...]
    pallas_call x1, Pallas kernels: 7.2 us -> 2.6 us  [block_sums(): pl.pallas_call(forward_kernel, in_specs=[smem, hbm, hbm] + [vmem] * 2, ou...]
    pallas_call x1, Pallas kernels: 60.2 us -> 62.8 us  [reduce_gather(): pl.pallas_call(reduce_gather_kernel, out_shape=(jax.ShapeDtypeStruct((512...]
where the time goes in v8:
time: 136 us
  Pallas kernels  134 us (99%)
  between operations  1.54 us (1%)
    pallas_call x1, Pallas kernels, reduce_gather(): pl.pallas_call(reduce_gather_kernel, out_shape=(jax.ShapeDtypeStruct((512...  62.8 us
    pallas_call x1, Pallas kernels, finish(): pl.pallas_call(finish_kernel, out_shape=(jax.ShapeDtypeStruct((512, 128),...  44.4 us
    pallas_call x1, Pallas kernels, prepare(): pl.pallas_call(prepare_kernel, out_shape=(jax.ShapeDtypeStruct((slots, 12...  21.3 us

profile of v8, /device:TPU:1, one launch (start us, length us, event | category | flops | bytes accessed | tf_op | source)
XLA Modules:
  0.0 135.9 jit_solution(16354040941696409207)
XLA Ops:
  1.3 21.3 %prepare.1 = (bf16[512,128,128]{2,1,0:T(8,128)(2,1)S(1)}, bf16[8,4,128,128]{3,2,1,0:T(8,128)(2,1)S(1)}) custom-call(s32[1,1]{1,0:T(1,128)S(6)} %copy.13.count_ref, s32[1,1,512,128]{3,2,1,0:T(8,128)} %off_hbm.1, bf16[1,1,512,128]{3,2,1,0:T(8,128)(2,1)} %w_hbm.1, bf16[512,128]{1,0:T(8,128)(2,1)} %feat_ref.1, bf16[128,128]{1,0:T(8,128)(2,1)} %weight_ref.1), custom_call_target="tpu_custom_call" | custom-call | tf_op jit(solution)/shard_map/prepare/pallas_call | solution.py:164
  22.5 0.0 copy-start.1
  22.6 0.0 copy-start.3
  22.6 2.6 %forward.1 = f32[128,128,128]{2,1,0:T(8,128)S(1)} custom-call(s32[1,1]{1,0:T(1,128)S(6)} %copy.13.count_ref, s32[1,1,512]{2,1,0:T(1,128)} %row_hbm.3, s32[1,1,512]{2,1,0:T(1,128)} %col_hbm.3, bf16[512,128,128]{2,1,0:T(8,128)(2,1)S(1)} %get-tuple-element.17.d_ref, bf16[32,128,128]{2,1,0:T(8,128)(2,1)S(1)} %bitcast.9), custom_call_target="tpu_custom_call" | custom-call | tf_op jit(solution)/shard_map/forward/pallas_call | solution.py:251
  25.2 0.0 copy-done.1
  25.2 0.0 copy-done.3
  25.2 62.8 %reduce_gather.1 = (bf16[512,128]{1,0:T(8,128)(2,1)S(1)}, bf16[4,2,4,512,128]{4,3,2,1,0:T(8,128)(2,1)S(1)}, f32[1,128]{1,0:T(1,128)S(1)}) custom-call(f32[4,2,4,512,128]{4,3,2,1,0:T(8,128)S(1)} %bitcast.6, f32[1,128]{1,0:T(1,128)S(1)} %bitcast.10, bf16[512,128]{1,0:T(8,128)(2,1)S(1)} %copy-done.1), custom_call_target="tpu_custom_call" | custom-call | tf_op jit(solution)/shard_map/reduce_gather/pallas_call | solution.py:567
  88.0 0.0 copy-start
  88.0 0.0 copy-start.2
  88.0 2.6 %backward.1 = (f32[32,128,128]{2,1,0:T(8,128)S(1)}, bf16[512,128]{1,0:T(8,128)(2,1)}) custom-call(s32[1,1]{1,0:T(1,128)S(6)} %copy.13.count_ref, s32[1,1,512]{2,1,0:T(1,128)} %row_hbm.3, s32[1,1,512]{2,1,0:T(1,128)} %col_hbm.3, bf16[512,128,128]{2,1,0:T(8,128)(2,1)S(1)} %get-tuple-element.17.d_ref, bf16[128,128,128]{2,1,0:T(8,128)(2,1)S(1)} %bitcast.7, ...), custom_call_target="tpu_custom_call" | custom-call | tf_op jit(solution)/shard_map/backward/pallas_call | solution.py:260
  90.6 0.0 copy-done
  90.6 0.0 copy-done.2
  90.6 44.4 %finish.1 = (bf16[512,128]{1,0:T(8,128)(2,1)S(1)}, f32[128,128]{1,0:T(8,128)S(1)}, f32[1,128]{1,0:T(1,128)S(1)}) custom-call(f32[4,2,512,128]{3,2,1,0:T(8,128)S(1)} %bitcast.8, bf16[512,128]{1,0:T(8,128)(2,1)S(1)} %copy-done, bf16[128,128]{1,0:T(8,128)(2,1)S(1)} %copy-done.2, f32[1,128]{1,0:T(1,128)S(1)} %get-tuple-element.23.bsum_ref), custom_call_target="tpu_custom_call" | custom-call | tf_op jit(solution)/shard_map/finish/pallas_call | solution.py:703
  135.1 0.7 export.1
Async XLA Ops:
  22.5 2.6 %copy-start.1 = (bf16[512,128]{1,0:T(8,128)(2,1)S(1)}, bf16[512,128]{1,0:T(8,128)(2,1)}, u32[]{:S(2)}) copy-start(bf16[512,128]{1,0:T(8,128)(2,1)} %cot_ref.1) | copy-start | bytes 393220
  22.6 2.6 %copy-start.3 = (f32[128]{0:T(128)S(1)}, f32[128]{0:T(128)}, u32[]{:S(2)}) copy-start(f32[128]{0:T(128)} %param.11) | copy-start | bytes 1540
  88.0 2.6 %copy-start = (bf16[512,128]{1,0:T(8,128)(2,1)S(1)}, bf16[512,128]{1,0:T(8,128)(2,1)}, u32[]{:S(2)}) copy-start(bf16[512,128]{1,0:T(8,128)(2,1)} %feat_ref.1) | copy-start | bytes 393220
  88.0 2.6 %copy-start.2 = (bf16[128,128]{1,0:T(8,128)(2,1)S(1)}, bf16[128,128]{1,0:T(8,128)(2,1)}, u32[]{:S(2)}) copy-start(bf16[128,128]{1,0:T(8,128)(2,1)} %weight_ref.1) | copy-start | bytes 98308
